TPU v7x, 512 devices: a whole 4x4x16 slice. The times are simulated.
512 devices in a mesh: dp: 32 (over z, core), shard: 16 (over y, x).
Axes of the slice: x: 4, y: 4, z: 16, core: 2. Of those that a mesh axis runs over, the one named last changes fastest.
Arguments:
- points: bfloat16 [131072, 1024], P(('dp', 'shard'))
- first_center: bfloat16 [1024], replicated, may hold values from -0.1875 to 0.1875
- counts: int32 [3, 32, 16], P(None, 'dp', 'shard'), may hold values from 0 to 4, as said below
- cand_index: int32 [3, 32, 16, 4], P(None, 'dp', 'shard'), may hold values from 0 to 255, as said below
Outputs:
- min_dist: float32 [131072], P(('dp', 'shard'))
- weights: float32 [131072], P(('dp', 'shard'))
- potentials: float32 [4], replicated
Inputs may be any that keep to these rules, and one draw needn't show every extreme that they name: In each round the counts of the 16 devices of one dp index sum to 16, so a round has 512 candidates; in each round and dp index some device has exactly 4. `cand_index`: each device's list in a round holds distinct local row numbers; only its first counts entries are candidates.
All inputs are finite; a program needn't handle non-finite values.
Results may differ from a plain program's by a relative error of at most 0.0003.
Values may be sent and summed in bfloat16 or wider, within the bound.
No kernel may reach another device: no remote copies, remote signals or barrier semaphores. Data moves between devices by JAX's collectives and lax.ppermute only.
A program may use at most 64 MiB of HBM per device.

v0:
```python
import jax
import jax.numpy as jnp
from jax import lax
from jax.experimental import pallas as pl
from jax.experimental.pallas import tpu as pltpu
from jax.sharding import Mesh
from jax.sharding import PartitionSpec as P


D = 1024
ROWS_DEV = 256
ROUNDS = 3
CAP = 4
ROWS = 131072
NZ, NC, NY, NXA, NXI = 16, 2, 4, 1, 4
PLANE = NY * NXA * NXI
FAR = NY * NXA
NEAR = NC * NXI
BLK = 16
CNT_ROW = ROUNDS * CAP
KEEP = ROUNDS * NZ

VMEM = pltpu.VMEM
SMEM = pltpu.SMEM
F32 = jnp.float32
BF16 = jnp.bfloat16


def iota(shape, dim):
    return lax.broadcasted_iota(jnp.int32, shape, dim)


def one_hot(cond):
    return jnp.where(cond, 1.0, 0.0).astype(BF16)


def dot_nt(a, b):
    return lax.dot_general(a, b, (((1,), (1,)), ((), ())), preferred_element_type=F32)


def pack_kernel(cnt_hbm, idx_hbm, pts_hbm, out_ref, cnt_ref, idx_ref, pts_ref, sem):
    fetch_idx = pltpu.make_async_copy(idx_hbm, idx_ref, sem.at[0])
    fetch_cnt = pltpu.make_async_copy(cnt_hbm, cnt_ref, sem.at[1])
    fetch = pltpu.make_async_copy(pts_hbm, pts_ref, sem.at[2])
    fetch_idx.start()
    fetch_cnt.start()
    fetch.start()
    fetch_idx.wait()
    fetch_cnt.wait()
    sub = iota((BLK, ROWS_DEV), 0)
    lane = iota((BLK, ROWS_DEV), 1)
    want = jnp.full((BLK, ROWS_DEV), -1, jnp.int32)
    for q in range(CNT_ROW):
        want = jnp.where(sub == q, idx_ref[q // CAP, 0, 0, q % CAP], want)
    fetch.wait()
    rows = jnp.dot(one_hot(lane == want), pts_ref[...], preferred_element_type=F32)
    sub = iota((BLK, D), 0)
    lane = iota((BLK, D), 1)
    for r in range(ROUNDS):
        here = jnp.logical_and(sub == CNT_ROW, lane == r)
        rows = jnp.where(here, cnt_ref[r].astype(F32), rows)
    rows = rows.astype(BF16)
    for i in range(PLANE):
        out_ref[i] = rows


def compact_kernel(recv_ref, out_ref):
    place = (lax.axis_index("y") * NXA + lax.axis_index("xa")) * NXI + lax.axis_index("xi")
    n = PLANE * BLK
    head = recv_ref[:, 0:128]
    src = iota((n, n), 0)
    dst = iota((n, n), 1)
    is_cnt = src % BLK == CNT_ROW
    own = one_hot(jnp.logical_and(is_cnt, src // BLK == dst // BLK))
    before = one_hot(jnp.logical_and(is_cnt, src // BLK < dst // BLK))
    contract = (((0,), (0,)), ((), ()))
    cnt = lax.dot_general(head, own, contract, preferred_element_type=F32)[:16]
    off = lax.dot_general(head, before, contract, preferred_element_type=F32)[:16]
    r = iota((16, n), 0)
    q = iota((16, n), 1) % BLK
    j = (q % CAP).astype(F32)
    live = jnp.logical_and(q < CNT_ROW, q // CAP == r)
    live = jnp.logical_and(live, j < cnt)
    live = jnp.logical_and(live, off + j == place.astype(F32))
    rows = jnp.dot(one_hot(live), recv_ref[...], preferred_element_type=F32)
    rows = rows[0:4].astype(BF16)
    for i in range(NZ):
        out_ref[i] = rows


def spread_kernel(recv_ref, out_ref, tmp_ref):
    for z in range(NZ):
        tmp_ref[4 * z : 4 * z + 4, :] = recv_ref[z].astype(F32)
    m = iota((KEEP, 4 * NZ), 0)
    k = iota((KEEP, 4 * NZ), 1)
    sel = one_hot(k == 4 * (m % NZ) + m // NZ)
    rows = jnp.dot(sel, tmp_ref[...].astype(BF16), preferred_element_type=F32)
    rows = rows.astype(BF16)
    for i in range(FAR):
        out_ref[i] = rows


def base_kernel(pts_ref, center_ref, out_ref):
    pts = pts_ref[...]
    wide = pts.astype(F32)
    sq = wide * wide
    hi = sq.astype(BF16)
    lo = (sq - hi.astype(F32)).astype(BF16)
    ones = jnp.ones((16, D), BF16)
    rows_norm = (dot_nt(ones, hi) + dot_nt(ones, lo))[0:1]
    center = jnp.broadcast_to(center_ref[...].reshape(1, D), (16, D))
    cwide = center.astype(F32)
    cnorm = jnp.sum(cwide * cwide, axis=1, keepdims=True)
    first = (cnorm - 2.0 * dot_nt(center, pts))[0:1]
    out_ref[0:1] = rows_norm
    out_ref[1:2] = jnp.maximum(rows_norm + first, 0.0)


def near_kernel(base_ref, cands_ref, *refs):
    *pts_refs, out_ref = refs
    cands = cands_ref[...]
    wide = cands.astype(F32)
    norm = jnp.sum(wide * wide, axis=1, keepdims=True)
    core = lax.axis_index("c")
    side = lax.axis_index("xi")
    for k, pts_ref in enumerate(pts_refs):
        block = (core + k // NXI) % NC * NXI + (side + k % NXI) % NXI
        prod = dot_nt(cands, pts_ref[...])
        val = (norm - 2.0 * prod).reshape(FAR, ROUNDS, NZ, ROWS_DEV)
        least = jnp.min(jnp.min(val, axis=0), axis=1)
        tail = jnp.zeros((8 - ROUNDS, ROWS_DEV), F32)
        if k == 0:
            tail = jnp.concatenate([base_ref[0:2], tail[2:]], axis=0)
        rows = jnp.concatenate([least, tail], axis=0)
        for i in range(NEAR):
            out_ref[i, block] = rows


def last_kernel(recv_ref, run_ref, sums_ref, all_ref):
    def base_row(row):
        return jnp.concatenate([recv_ref[b, b, row : row + 1] for b in range(NEAR)], axis=0)

    rows_norm = base_row(ROUNDS)
    running = base_row(ROUNDS + 1)
    lane = iota((FAR, 128), 1)
    sums = jnp.where(lane == 0, jnp.sum(running), 0.0)
    for r in range(ROUNDS):
        least = recv_ref[0, :, r]
        for s in range(1, NEAR):
            least = jnp.minimum(least, recv_ref[s, :, r])
        running = jnp.minimum(running, jnp.maximum(rows_norm + least, 0.0))
        sums = jnp.where(lane == r + 1, jnp.sum(running), sums)
    for b in range(NEAR):
        all_ref[b] = running[b : b + 1]
    run_ref[...] = all_ref[lax.axis_index("c") * NXI + lax.axis_index("xi")]
    sums_ref[...] = sums


def relay_kernel(recv_ref, out_ref):
    total = jnp.sum(recv_ref[...], axis=0, keepdims=True)
    out_ref[...] = jnp.broadcast_to(total, (NZ, 128))


def final_kernel(recv_ref, run_ref, dist_ref, weight_ref, pot_ref):
    total = jnp.sum(recv_ref[...], axis=0, keepdims=True)
    lane = iota((1, 128), 1)
    last = jnp.sum(jnp.where(lane == ROUNDS, total, 0.0), axis=1, keepdims=True)
    running = run_ref[...]
    dist_ref[...] = running.reshape(ROWS_DEV)
    weight_ref[...] = (running * (ROWS / last)).reshape(ROWS_DEV)
    pot_ref[...] = total.reshape(128)[0 : ROUNDS + 1]


def vspec():
    return pl.BlockSpec(memory_space=VMEM)


def call(kernel, ins, outs, scratch=(), near=True):
    shapes = [VMEM(s, d) if near else jax.ShapeDtypeStruct(s, d) for s, d in outs]
    single = len(shapes) == 1
    kern = pl.pallas_call(
        kernel,
        in_specs=ins,
        out_specs=vspec() if single else [vspec() for _ in shapes],
        out_shape=shapes[0] if single else shapes,
        scratch_shapes=list(scratch),
        compiler_params=pltpu.CompilerParams(vmem_limit_bytes=16 << 20),
    )

    def run(*args):
        placed = []
        for a, i in zip(args, ins):
            space = VMEM if i.memory_space == VMEM else pltpu.HBM
            placed.append(pltpu.with_memory_space_constraint(a, space))
        return kern(*placed)

    return run


def body(points, first_center, counts, cand_index):
    pack = call(
        pack_kernel,
        [pl.BlockSpec(memory_space=pl.ANY)] * 3,
        [((PLANE, BLK, D), BF16)],
        [
            SMEM((ROUNDS,), jnp.int32),
            SMEM((ROUNDS, 1, 1, CAP), jnp.int32),
            VMEM((ROWS_DEV, D), BF16),
            pltpu.SemaphoreType.DMA((3,)),
        ],
    )
    blocks = pack(counts.reshape(ROUNDS), cand_index, points)
    plane = ("y", "xa", "xi")
    far = ("y", "xa")
    blocks, early = lax.optimization_barrier((blocks, points))
    blocks = lax.all_to_all(blocks, plane, 0, 0)
    compact = call(compact_kernel, [vspec()], [((NZ, 4, D), BF16)])
    mine = compact(blocks.reshape(PLANE * BLK, D))
    mine, shared = lax.optimization_barrier((mine, points))
    mine = lax.all_to_all(mine, "z", 0, 0)

    def from_side(rows, k):
        return lax.ppermute(rows, "xi", [((i + k) % NXI, i) for i in range(NXI)])

    def swap(rows):
        return lax.ppermute(rows, "c", [(0, 1), (1, 0)])

    here = [points, from_side(early, 1), from_side(shared, 2), from_side(early, 3)]
    there = [swap(p) for p in here]
    base = call(base_kernel, [vspec()] * 2, [((2, ROWS_DEV), F32)])(points, first_center)
    spread = call(spread_kernel, [vspec()], [((FAR, KEEP, D), BF16)], [VMEM((4 * NZ, D), F32)])
    cands = lax.all_to_all(spread(mine), far, 0, 0).reshape(FAR * KEEP, D)
    near = call(near_kernel, [vspec()] * (2 + NEAR), [((NEAR, NEAR, 8, ROWS_DEV), F32)])
    mins = lax.all_to_all(near(base, cands, *here, *there), ("c", "xi"), 0, 0)
    last = call(
        last_kernel,
        [vspec()],
        [((1, ROWS_DEV), F32), ((FAR, 128), F32)],
        [VMEM((NEAR, 1, ROWS_DEV), F32)],
    )
    running, sums = last(mins)
    sums = lax.all_to_all(sums, far, 0, 0)
    relay = call(relay_kernel, [vspec()], [((NZ, 128), F32)])
    sums = lax.all_to_all(relay(sums), "z", 0, 0)
    final = call(
        final_kernel,
        [vspec()] * 2,
        [((ROWS_DEV,), F32), ((ROWS_DEV,), F32), ((ROUNDS + 1,), F32)],
        near=False,
    )
    return tuple(final(sums, running))


def solution(mesh):
    axes = ("z", "c", "y", "xa", "xi")
    plane = ("y", "xa", "xi")
    grid = Mesh(mesh.devices.reshape(NZ, NC, NY, NXA, NXI), axes)
    placed = (P(axes, None), P(), P(None, ("z", "c"), plane), P(None, ("z", "c"), plane, None))


    return jax.shard_map(
        body,
        mesh=grid,
        in_specs=placed,
        out_specs=(P(axes), P(axes), P()),
        check_vma=False,
    )
```

profile of v0, /device:TPU:1, one launch (start us, length us, event | category | flops | bytes accessed | tf_op | source)
XLA Modules:
  0.0 111.2 jit_solution(11018765000446395002)
XLA Ops:
  0.6 2.1 %shard_map.68 = bf16[16,16,1024]{2,1,0:T(8,128)(2,1)} custom-call(s32[3]{0:T(128)} %bitcast.17, s32[3,1,1,4]{3,2,1,0:T(1,128)} %idx_hbm.1, bf16[256,1024]{1,0:T(8,128)(2,1)} %refs_0_.1), custom_call_target="tpu_custom_call" | custom-call | tf_op jit(solution)/shard_map/pallas_call | solution.py:195
  2.7 0.0 copy-start
  2.7 7.7 %all-to-all-start = ((bf16[16,16,1024]{2,1,0:T(8,128)(2,1)}), bf16[16,16,1024]{2,1,0:T(8,128)(2,1)S(1)}, u32[]{:S(2)}, u32[]{:S(2)}) async-start(bf16[16,16,1024]{2,1,0:T(8,128)(2,1)} %shard_map.68), calls=%async_computation | async-start | bytes 1048576 | tf_op jit(solution)/shard_map/all_to_all | solution.py:216
  10.4 0.0 copy-done
  10.5 3.3 %collective-permute-start.2 = (bf16[256,1024]{1,0:T(8,128)(2,1)S(1)}, bf16[256,1024]{1,0:T(8,128)(2,1)S(1)}, u32[]{:S(2)}, u32[]{:S(2)}) collective-permute-start(bf16[256,1024]{1,0:T(8,128)(2,1)S(1)} %copy-done), channel_id=1, source_target_pairs={{3,0},{0,1},{1,2},{2,3},{7,4},{4,5},{5,6},{6,7},{11,8},{8,9},{9,10... | collective-permute-start | bytes 1572872 | tf_op jit(solution)/shard_map/ppermute | solution.py:223
  13.7 3.2 %collective-permute-start = (bf16[256,1024]{1,0:T(8,128)(2,1)S(1)}, bf16[256,1024]{1,0:T(8,128)(2,1)S(1)}, u32[]{:S(2)}, u32[]{:S(2)}) collective-permute-start(bf16[256,1024]{1,0:T(8,128)(2,1)S(1)} %copy-done), channel_id=1, source_target_pairs={{1,0},{2,1},{3,2},{0,3},{5,4},{6,5},{7,6},{4,7},{9,8},{10,9},{11,1... | collective-permute-start | bytes 1572872 | tf_op jit(solution)/shard_map/ppermute | solution.py:223
  17.0 2.7 %all-to-all-done = bf16[16,16,1024]{2,1,0:T(8,128)(2,1)S(1)} async-done(((bf16[16,16,1024]{2,1,0:T(8,128)(2,1)}), bf16[16,16,1024]{2,1,0:T(8,128)(2,1)S(1)}, u32[]{:S(2)}, u32[]{:S(2)}) %all-to-all-start) | async-done | bytes 524320 | tf_op jit(solution)/shard_map/all_to_all | solution.py:216
  19.6 1.0 shard_map.69
  20.6 2.2 %collective-permute-start.1 = (bf16[256,1024]{1,0:T(8,128)(2,1)S(1)}, bf16[256,1024]{1,0:T(8,128)(2,1)S(1)}, u32[]{:S(2)}, u32[]{:S(2)}) collective-permute-start(bf16[256,1024]{1,0:T(8,128)(2,1)S(1)} %copy-done), channel_id=1, source_target_pairs={{2,0},{3,1},{0,2},{1,3},{6,4},{7,5},{4,6},{5,7},{10,8},{11,9},{8,1... | collective-permute-start | bytes 1572872 | tf_op jit(solution)/shard_map/ppermute | solution.py:223
  22.8 16.3 %all-to-all-start.1 = ((bf16[16,4,1024]{2,1,0:T(4,128)(2,1)}), bf16[16,4,1024]{2,1,0:T(4,128)(2,1)S(1)}, u32[]{:S(2)}, u32[]{:S(2)}) async-start(bf16[16,4,1024]{2,1,0:T(4,128)(2,1)} %shard_map.69), calls=%async_computation.1 | async-start | bytes 262144 | tf_op jit(solution)/shard_map/all_to_all | solution.py:220
  39.2 5.1 %collective-permute-start.3 = (bf16[256,1024]{1,0:T(8,128)(2,1)S(1)}, bf16[256,1024]{1,0:T(8,128)(2,1)S(1)}, u32[]{:S(2)}, u32[]{:S(2)}) collective-permute-start(bf16[256,1024]{1,0:T(8,128)(2,1)S(1)} %copy-done), channel_id=1, source_target_pairs={{0,16},{16,0},{1,17},{17,1},{2,18},{18,2},{3,19},{19,3},{4,20},{20... | collective-permute-start | bytes 1572872 | tf_op jit(solution)/shard_map/ppermute | solution.py:226
  44.3 0.0 collective-permute-done.2.refs_3_
  44.3 1.9 %collective-permute-start.6 = (bf16[256,1024]{1,0:T(8,128)(2,1)S(1)}, bf16[256,1024]{1,0:T(8,128)(2,1)}, u32[]{:S(2)}, u32[]{:S(2)}) collective-permute-start(bf16[256,1024]{1,0:T(8,128)(2,1)S(1)} %collective-permute-done.2.refs_3_), channel_id=1, source_target_pairs={{0,16},{16,0},{1,17},{17,1},{2,18},{18,2},{3,19},{19,3},{4,20},{20... | collective-permute-start | bytes 1572872 | tf_op jit(solution)/shard_map/ppermute | solution.py:226
  46.3 0.0 collective-permute-done.refs_1_
  46.3 2.4 %collective-permute-start.4 = (bf16[256,1024]{1,0:T(8,128)(2,1)S(1)}, bf16[256,1024]{1,0:T(8,128)(2,1)}, u32[]{:S(2)}, u32[]{:S(2)}) collective-permute-start(bf16[256,1024]{1,0:T(8,128)(2,1)S(1)} %collective-permute-done.refs_1_), channel_id=1, source_target_pairs={{0,16},{16,0},{1,17},{17,1},{2,18},{18,2},{3,19},{19,3},{4,20},{20... | collective-permute-start | bytes 1572872 | tf_op jit(solution)/shard_map/ppermute | solution.py:226
  48.7 0.0 collective-permute-done.1.refs_2_
  48.7 1.9 %collective-permute-start.5 = (bf16[256,1024]{1,0:T(8,128)(2,1)S(1)}, bf16[256,1024]{1,0:T(8,128)(2,1)}, u32[]{:S(2)}, u32[]{:S(2)}) collective-permute-start(bf16[256,1024]{1,0:T(8,128)(2,1)S(1)} %collective-permute-done.1.refs_2_), channel_id=1, source_target_pairs={{0,16},{16,0},{1,17},{17,1},{2,18},{18,2},{3,19},{19,3},{4,20},{20... | collective-permute-start | bytes 1572872 | tf_op jit(solution)/shard_map/ppermute | solution.py:226
  50.6 0.5 all-to-all-done.1.recv_ref
  51.1 0.9 shard_map.70
  52.1 0.0 copy-start.1
  52.1 3.6 %all-to-all-start.2 = ((bf16[4,48,1024]{2,1,0:T(8,128)(2,1)}), bf16[4,48,1024]{2,1,0:T(8,128)(2,1)S(1)}, u32[]{:S(2)}, u32[]{:S(2)}) async-start(bf16[4,48,1024]{2,1,0:T(8,128)(2,1)} %shard_map.70), calls=%async_computation.2 | async-start | bytes 786432 | tf_op jit(solution)/shard_map/all_to_all | solution.py:232
  55.7 0.0 copy-done.1
  55.7 0.6 shard_map.67.base_ref
  56.2 0.0 collective-permute-done.3.refs_4_
  56.2 0.0 collective-permute-done.6.refs_7_
  56.3 0.0 collective-permute-done.4.refs_5_
  56.3 5.6 %all-to-all-done.2 = bf16[4,48,1024]{2,1,0:T(8,128)(2,1)S(1)} async-done(((bf16[4,48,1024]{2,1,0:T(8,128)(2,1)}), bf16[4,48,1024]{2,1,0:T(8,128)(2,1)S(1)}, u32[]{:S(2)}, u32[]{:S(2)}) %all-to-all-start.2) | async-done | bytes 393248 | tf_op jit(solution)/shard_map/all_to_all | solution.py:232
  61.9 0.0 collective-permute-done.5.refs_6_
  61.9 2.9 %shard_map.71 = f32[8,8,8,256]{3,2,1,0:T(8,128)S(1)} custom-call(f32[2,256]{1,0:T(2,128)S(1)} %shard_map.67.base_ref, bf16[192,1024]{1,0:T(8,128)(2,1)S(1)} %bitcast.12, bf16[256,1024]{1,0:T(8,128)(2,1)S(1)} %copy-done, bf16[256,1024]{1,0:T(8,128)(2,1)S(1)} %collective-permute-done.refs_1_, bf16[256,1024]{1,0:T(8,128)(2,1)S(1)} %collective-permute-done.1.refs_2_, ...), custom_call_target="tpu_custom_call" | custom-call | tf_op jit(solution)/shard_map/pallas_call | solution.py:195
  64.8 19.4 %all_to_all.42.recv_ref = f32[8,8,8,256]{3,2,1,0:T(8,128)S(1)} all-to-all(f32[8,8,8,256]{3,2,1,0:T(8,128)S(1)} %shard_map.71), channel_id=1, replica_groups=mesh['z'=16,'c'=2,'y'=4,'xa'=1,'xi'=4] {'c','xi'}, dimensions={0} | all-to-all | bytes 1048576 | tf_op jit(solution)/shard_map/all_to_all | solution.py:234
  84.3 0.2 shard_map.72
  84.5 6.5 %all_to_all.43 = f32[4,1,128]{2,1,0:T(1,128)S(1)} all-to-all(f32[4,1,128]{2,1,0:T(1,128)S(1)} %bitcast.16), channel_id=1, replica_groups=mesh['z'=16,'c'=2,'y'=4,'xa'=1,'xi'=4] {'y','xa'}, dimensions={0} | all-to-all | bytes 4096 | tf_op jit(solution)/shard_map/all_to_all | solution.py:242
  90.9 19.6 %all_to_all.44 = f32[16,1,128]{2,1,0:T(1,128)S(1)} all-to-all(f32[16,1,128]{2,1,0:T(1,128)S(1)} %bitcast.13), channel_id=1, replica_groups=mesh['z'=16,'c'=2,'y'=4,'xa'=1,'xi'=4] {'z'}, dimensions={0} | all-to-all | bytes 16384 | tf_op jit(solution)/shard_map/all_to_all | solution.py:244
  110.6 0.7 shard_map.74
  (1 shorter events, 0.0 us)
Async XLA Ops:
  2.7 7.7 %copy-start = (bf16[256,1024]{1,0:T(8,128)(2,1)S(1)}, bf16[256,1024]{1,0:T(8,128)(2,1)}, u32[]{:S(2)}) copy-start(bf16[256,1024]{1,0:T(8,128)(2,1)} %refs_0_.1) | copy-start | bytes 1572868
  2.7 16.9 %all-to-all-start = ((bf16[16,16,1024]{2,1,0:T(8,128)(2,1)}), bf16[16,16,1024]{2,1,0:T(8,128)(2,1)S(1)}, u32[]{:S(2)}, u32[]{:S(2)}) async-start(bf16[16,16,1024]{2,1,0:T(8,128)(2,1)} %shard_map.68), calls=%async_computation | async-start | bytes 1048576 | tf_op jit(solution)/shard_map/all_to_all | solution.py:216
  10.5 33.9 %collective-permute-start.2 = (bf16[256,1024]{1,0:T(8,128)(2,1)S(1)}, bf16[256,1024]{1,0:T(8,128)(2,1)S(1)}, u32[]{:S(2)}, u32[]{:S(2)}) collective-permute-start(bf16[256,1024]{1,0:T(8,128)(2,1)S(1)} %copy-done), channel_id=1, source_target_pairs={{3,0},{0,1},{1,2},{2,3},{7,4},{4,5},{5,6},{6,7},{11,8},{8,9},{9,10... | collective-permute-start | bytes 1572872 | tf_op jit(solution)/shard_map/ppermute | solution.py:223
  13.7 32.5 %collective-permute-start = (bf16[256,1024]{1,0:T(8,128)(2,1)S(1)}, bf16[256,1024]{1,0:T(8,128)(2,1)S(1)}, u32[]{:S(2)}, u32[]{:S(2)}) collective-permute-start(bf16[256,1024]{1,0:T(8,128)(2,1)S(1)} %copy-done), channel_id=1, source_target_pairs={{1,0},{2,1},{3,2},{0,3},{5,4},{6,5},{7,6},{4,7},{9,8},{10,9},{11,1... | collective-permute-start | bytes 1572872 | tf_op jit(solution)/shard_map/ppermute | solution.py:223
  20.6 28.1 %collective-permute-start.1 = (bf16[256,1024]{1,0:T(8,128)(2,1)S(1)}, bf16[256,1024]{1,0:T(8,128)(2,1)S(1)}, u32[]{:S(2)}, u32[]{:S(2)}) collective-permute-start(bf16[256,1024]{1,0:T(8,128)(2,1)S(1)} %copy-done), channel_id=1, source_target_pairs={{2,0},{3,1},{0,2},{1,3},{6,4},{7,5},{4,6},{5,7},{10,8},{11,9},{8,1... | collective-permute-start | bytes 1572872 | tf_op jit(solution)/shard_map/ppermute | solution.py:223
  22.8 28.3 %all-to-all-start.1 = ((bf16[16,4,1024]{2,1,0:T(4,128)(2,1)}), bf16[16,4,1024]{2,1,0:T(4,128)(2,1)S(1)}, u32[]{:S(2)}, u32[]{:S(2)}) async-start(bf16[16,4,1024]{2,1,0:T(4,128)(2,1)} %shard_map.69), calls=%async_computation.1 | async-start | bytes 262144 | tf_op jit(solution)/shard_map/all_to_all | solution.py:220
  39.2 17.1 %collective-permute-start.3 = (bf16[256,1024]{1,0:T(8,128)(2,1)S(1)}, bf16[256,1024]{1,0:T(8,128)(2,1)S(1)}, u32[]{:S(2)}, u32[]{:S(2)}) collective-permute-start(bf16[256,1024]{1,0:T(8,128)(2,1)S(1)} %copy-done), channel_id=1, source_target_pairs={{0,16},{16,0},{1,17},{17,1},{2,18},{18,2},{3,19},{19,3},{4,20},{20... | collective-permute-start | bytes 1572872 | tf_op jit(solution)/shard_map/ppermute | solution.py:226
  44.3 11.9 %collective-permute-start.6 = (bf16[256,1024]{1,0:T(8,128)(2,1)S(1)}, bf16[256,1024]{1,0:T(8,128)(2,1)}, u32[]{:S(2)}, u32[]{:S(2)}) collective-permute-start(bf16[256,1024]{1,0:T(8,128)(2,1)S(1)} %collective-permute-done.2.refs_3_), channel_id=1, source_target_pairs={{0,16},{16,0},{1,17},{17,1},{2,18},{18,2},{3,19},{19,3},{4,20},{20... | collective-permute-start | bytes 1572872 | tf_op jit(solution)/shard_map/ppermute | solution.py:226
  46.3 10.0 %collective-permute-start.4 = (bf16[256,1024]{1,0:T(8,128)(2,1)S(1)}, bf16[256,1024]{1,0:T(8,128)(2,1)}, u32[]{:S(2)}, u32[]{:S(2)}) collective-permute-start(bf16[256,1024]{1,0:T(8,128)(2,1)S(1)} %collective-permute-done.refs_1_), channel_id=1, source_target_pairs={{0,16},{16,0},{1,17},{17,1},{2,18},{18,2},{3,19},{19,3},{4,20},{20... | collective-permute-start | bytes 1572872 | tf_op jit(solution)/shard_map/ppermute | solution.py:226
  48.7 13.2 %collective-permute-start.5 = (bf16[256,1024]{1,0:T(8,128)(2,1)S(1)}, bf16[256,1024]{1,0:T(8,128)(2,1)}, u32[]{:S(2)}, u32[]{:S(2)}) collective-permute-start(bf16[256,1024]{1,0:T(8,128)(2,1)S(1)} %collective-permute-done.1.refs_2_), channel_id=1, source_target_pairs={{0,16},{16,0},{1,17},{17,1},{2,18},{18,2},{3,19},{19,3},{4,20},{20... | collective-permute-start | bytes 1572872 | tf_op jit(solution)/shard_map/ppermute | solution.py:226
  52.1 3.6 %copy-start.1 = (bf16[1024]{0:T(1024)(128)(2,1)S(1)}, bf16[1024]{0:T(1024)(128)(2,1)}, u32[]{:S(2)}) copy-start(bf16[1024]{0:T(1024)(128)(2,1)} %center_ref.1) | copy-start | bytes 6148
  52.1 9.8 %all-to-all-start.2 = ((bf16[4,48,1024]{2,1,0:T(8,128)(2,1)}), bf16[4,48,1024]{2,1,0:T(8,128)(2,1)S(1)}, u32[]{:S(2)}, u32[]{:S(2)}) async-start(bf16[4,48,1024]{2,1,0:T(8,128)(2,1)} %shard_map.70), calls=%async_computation.2 | async-start | bytes 786432 | tf_op jit(solution)/shard_map/all_to_all | solution.py:232
where the time goes:
time: 113 us; the launch traced here: 111 us
  starting transfers between devices  47.7 us (42%)
  blocking collectives  45.6 us (40%)
  waiting for transfers between devices  8.78 us (8%)
  Pallas kernels  8.33 us (7%)
    all_to_all x1, blocking collectives, body(): sums = lax.all_to_all(relay(sums), 'z', 0, 0)  19.6 us
    all_to_all x1, blocking collectives, body(): mins = lax.all_to_all(near(base, cands, *here, *there), ('c', 'xi'), 0, 0)  19.4 us
    all_to_all x1, starting transfers between devices, body(): mine = lax.all_to_all(mine, 'z', 0, 0)  16.3 us
    ppermute x4, starting transfers between devices, swap(): return lax.ppermute(rows, 'c', [(0, 1), (1, 0)])  11.4 us
    ppermute x3, starting transfers between devices, from_side(): return lax.ppermute(rows, 'xi', [((i + k) % NXI, i) for i in range(NXI)])  8.72 us
    pallas_call x8, Pallas kernels, run(): return kern(*placed)  8.33 us
    all_to_all x1, starting transfers between devices, body(): blocks = lax.all_to_all(blocks, plane, 0, 0)  7.72 us
    all_to_all x1, blocking collectives, body(): sums = lax.all_to_all(sums, far, 0, 0)  6.47 us
  transfers between devices with their start and end apart: 10, of which 3 were waited for; matrix products, arithmetic and copies ran while one was open for 0% of the time, Pallas kernels for 2%

commit v1 on v0

--- a/solution.py
+++ b/solution.py
@@ -117,37 +117,48 @@
 
 
 def near_kernel(base_ref, cands_ref, *refs):
-    *pts_refs, out_ref = refs
+    here = refs[:NXI]
+    there = refs[NXI:NEAR]
+    out_ref, got_ref, rows_ref, sem = refs[NEAR:]
+    fetches = [pltpu.make_async_copy(src, got_ref.at[k], sem.at[k]) for k, src in enumerate(there)]
+    for fetch in fetches:
+        fetch.start()
     cands = cands_ref[...]
     wide = cands.astype(F32)
     norm = jnp.sum(wide * wide, axis=1, keepdims=True)
     core = lax.axis_index("c")
     side = lax.axis_index("xi")
-    for k, pts_ref in enumerate(pts_refs):
+    for k in range(NEAR):
         block = (core + k // NXI) % NC * NXI + (side + k % NXI) % NXI
-        prod = dot_nt(cands, pts_ref[...])
-        val = (norm - 2.0 * prod).reshape(FAR, ROUNDS, NZ, ROWS_DEV)
+        if k < NXI:
+            pts = here[k][...]
+        else:
+            fetches[k - NXI].wait()
+            pts = got_ref[k - NXI]
+        val = (norm - 2.0 * dot_nt(cands, pts)).reshape(FAR, ROUNDS, NZ, ROWS_DEV)
         least = jnp.min(jnp.min(val, axis=0), axis=1)
-        tail = jnp.zeros((8 - ROUNDS, ROWS_DEV), F32)
-        if k == 0:
-            tail = jnp.concatenate([base_ref[0:2], tail[2:]], axis=0)
-        rows = jnp.concatenate([least, tail], axis=0)
-        for i in range(NEAR):
-            out_ref[i, block] = rows
+        for r in range(ROUNDS):
+            rows_ref[pl.ds(r * NEAR + block, 1), :] = least[r : r + 1]
+    rows_ref[ROUNDS * NEAR : ROUNDS * NEAR + 2, :] = base_ref[...]
+    rows_ref[ROUNDS * NEAR + 2 :, :] = jnp.zeros((NEAR - 2, ROWS_DEV), F32)
+    rows = rows_ref[...]
+    for i in range(NEAR):
+        out_ref[i] = rows
 
 
 def last_kernel(recv_ref, run_ref, sums_ref, all_ref):
     def base_row(row):
-        return jnp.concatenate([recv_ref[b, b, row : row + 1] for b in range(NEAR)], axis=0)
-
-    rows_norm = base_row(ROUNDS)
-    running = base_row(ROUNDS + 1)
+        row += ROUNDS * NEAR
+        return jnp.concatenate([recv_ref[b, row : row + 1] for b in range(NEAR)], axis=0)
+
+    rows_norm = base_row(0)
+    running = base_row(1)
     lane = iota((FAR, 128), 1)
     sums = jnp.where(lane == 0, jnp.sum(running), 0.0)
     for r in range(ROUNDS):
-        least = recv_ref[0, :, r]
+        least = recv_ref[0, r * NEAR : (r + 1) * NEAR]
         for s in range(1, NEAR):
-            least = jnp.minimum(least, recv_ref[s, :, r])
+            least = jnp.minimum(least, recv_ref[s, r * NEAR : (r + 1) * NEAR])
         running = jnp.minimum(running, jnp.maximum(rows_norm + least, 0.0))
         sums = jnp.where(lane == r + 1, jnp.sum(running), sums)
     for b in range(NEAR):
@@ -230,7 +241,16 @@
     base = call(base_kernel, [vspec()] * 2, [((2, ROWS_DEV), F32)])(points, first_center)
     spread = call(spread_kernel, [vspec()], [((FAR, KEEP, D), BF16)], [VMEM((4 * NZ, D), F32)])
     cands = lax.all_to_all(spread(mine), far, 0, 0).reshape(FAR * KEEP, D)
-    near = call(near_kernel, [vspec()] * (2 + NEAR), [((NEAR, NEAR, 8, ROWS_DEV), F32)])
+    near = call(
+        near_kernel,
+        [vspec()] * (2 + NXI) + [pl.BlockSpec(memory_space=pl.ANY)] * NXI,
+        [((NEAR, 4 * NEAR, ROWS_DEV), F32)],
+        [
+            VMEM((NXI, ROWS_DEV, D), BF16),
+            VMEM((4 * NEAR, ROWS_DEV), F32),
+            pltpu.SemaphoreType.DMA((NXI,)),
+        ],
+    )
     mins = lax.all_to_all(near(base, cands, *here, *there), ("c", "xi"), 0, 0)
     last = call(
         last_kernel,

time: 113 us -> 111 us (0.982)
  blocking collectives: 45.6 us -> 42.8 us
    all_to_all x1, blocking collectives: 19.4 us -> 16.6 us  [body(): mins = lax.all_to_all(near(base, cands, *here, *there), ('c', 'xi'), 0, 0)]
where the time goes in v1:
time: 111 us; the launch traced here: 109 us
  starting transfers between devices  47.7 us (43%)
  blocking collectives  42.8 us (39%)
  Pallas kernels  8.96 us (8%)
  waiting for transfers between devices  8.77 us (8%)
    all_to_all x1, blocking collectives, body(): sums = lax.all_to_all(relay(sums), 'z', 0, 0)  19.6 us
    all_to_all x1, blocking collectives, body(): mins = lax.all_to_all(near(base, cands, *here, *there), ('c', 'xi'), 0, 0)  16.6 us
    all_to_all x1, starting transfers between devices, body(): mine = lax.all_to_all(mine, 'z', 0, 0)  16.3 us
    ppermute x4, starting transfers between devices, swap(): return lax.ppermute(rows, 'c', [(0, 1), (1, 0)])  11.4 us
    pallas_call x8, Pallas kernels, run(): return kern(*placed)  8.96 us
    ppermute x3, starting transfers between devices, from_side(): return lax.ppermute(rows, 'xi', [((i + k) % NXI, i) for i in range(NXI)])  8.72 us
    all_to_all x1, starting transfers between devices, body(): blocks = lax.all_to_all(blocks, plane, 0, 0)  7.72 us
    all_to_all x1, blocking collectives, body(): sums = lax.all_to_all(sums, far, 0, 0)  6.47 us
  transfers between devices with their start and end apart: 10, of which 3 were waited for; matrix products, arithmetic and copies ran while one was open for 0% of the time, Pallas kernels for 2%

profile of v1, /device:TPU:1, one launch (start us, length us, event | category | flops | bytes accessed | tf_op | source)
XLA Modules:
  0.0 109.1 jit_solution(16587143259876251912)
XLA Ops:
  0.6 2.1 %shard_map.68 = bf16[16,16,1024]{2,1,0:T(8,128)(2,1)} custom-call(s32[3]{0:T(128)} %bitcast.17, s32[3,1,1,4]{3,2,1,0:T(1,128)} %idx_hbm.1, bf16[256,1024]{1,0:T(8,128)(2,1)} %refs_0_.1), custom_call_target="tpu_custom_call" | custom-call | tf_op jit(solution)/shard_map/pallas_call | solution.py:206
  2.7 0.0 copy-start
  2.7 7.7 %all-to-all-start = ((bf16[16,16,1024]{2,1,0:T(8,128)(2,1)}), bf16[16,16,1024]{2,1,0:T(8,128)(2,1)S(1)}, u32[]{:S(2)}, u32[]{:S(2)}) async-start(bf16[16,16,1024]{2,1,0:T(8,128)(2,1)} %shard_map.68), calls=%async_computation | async-start | bytes 1048576 | tf_op jit(solution)/shard_map/all_to_all | solution.py:227
  10.4 0.0 copy-done
  10.5 3.3 %collective-permute-start.2 = (bf16[256,1024]{1,0:T(8,128)(2,1)S(1)}, bf16[256,1024]{1,0:T(8,128)(2,1)S(1)}, u32[]{:S(2)}, u32[]{:S(2)}) collective-permute-start(bf16[256,1024]{1,0:T(8,128)(2,1)S(1)} %copy-done), channel_id=1, source_target_pairs={{3,0},{0,1},{1,2},{2,3},{7,4},{4,5},{5,6},{6,7},{11,8},{8,9},{9,10... | collective-permute-start | bytes 1572872 | tf_op jit(solution)/shard_map/ppermute | solution.py:234
  13.7 3.2 %collective-permute-start = (bf16[256,1024]{1,0:T(8,128)(2,1)S(1)}, bf16[256,1024]{1,0:T(8,128)(2,1)S(1)}, u32[]{:S(2)}, u32[]{:S(2)}) collective-permute-start(bf16[256,1024]{1,0:T(8,128)(2,1)S(1)} %copy-done), channel_id=1, source_target_pairs={{1,0},{2,1},{3,2},{0,3},{5,4},{6,5},{7,6},{4,7},{9,8},{10,9},{11,1... | collective-permute-start | bytes 1572872 | tf_op jit(solution)/shard_map/ppermute | solution.py:234
  17.0 2.7 %all-to-all-done = bf16[16,16,1024]{2,1,0:T(8,128)(2,1)S(1)} async-done(((bf16[16,16,1024]{2,1,0:T(8,128)(2,1)}), bf16[16,16,1024]{2,1,0:T(8,128)(2,1)S(1)}, u32[]{:S(2)}, u32[]{:S(2)}) %all-to-all-start) | async-done | bytes 524320 | tf_op jit(solution)/shard_map/all_to_all | solution.py:227
  19.6 1.0 shard_map.69
  20.6 2.2 %collective-permute-start.1 = (bf16[256,1024]{1,0:T(8,128)(2,1)S(1)}, bf16[256,1024]{1,0:T(8,128)(2,1)S(1)}, u32[]{:S(2)}, u32[]{:S(2)}) collective-permute-start(bf16[256,1024]{1,0:T(8,128)(2,1)S(1)} %copy-done), channel_id=1, source_target_pairs={{2,0},{3,1},{0,2},{1,3},{6,4},{7,5},{4,6},{5,7},{10,8},{11,9},{8,1... | collective-permute-start | bytes 1572872 | tf_op jit(solution)/shard_map/ppermute | solution.py:234
  22.9 16.3 %all-to-all-start.1 = ((bf16[16,4,1024]{2,1,0:T(4,128)(2,1)}), bf16[16,4,1024]{2,1,0:T(4,128)(2,1)S(1)}, u32[]{:S(2)}, u32[]{:S(2)}) async-start(bf16[16,4,1024]{2,1,0:T(4,128)(2,1)} %shard_map.69), calls=%async_computation.1 | async-start | bytes 262144 | tf_op jit(solution)/shard_map/all_to_all | solution.py:231
  39.2 5.1 %collective-permute-start.3 = (bf16[256,1024]{1,0:T(8,128)(2,1)S(1)}, bf16[256,1024]{1,0:T(8,128)(2,1)S(1)}, u32[]{:S(2)}, u32[]{:S(2)}) collective-permute-start(bf16[256,1024]{1,0:T(8,128)(2,1)S(1)} %copy-done), channel_id=1, source_target_pairs={{0,16},{16,0},{1,17},{17,1},{2,18},{18,2},{3,19},{19,3},{4,20},{20... | collective-permute-start | bytes 1572872 | tf_op jit(solution)/shard_map/ppermute | solution.py:237
  44.3 0.0 collective-permute-done.2.refs_3_
  44.4 1.9 %collective-permute-start.6 = (bf16[256,1024]{1,0:T(8,128)(2,1)S(1)}, bf16[256,1024]{1,0:T(8,128)(2,1)}, u32[]{:S(2)}, u32[]{:S(2)}) collective-permute-start(bf16[256,1024]{1,0:T(8,128)(2,1)S(1)} %collective-permute-done.2.refs_3_), channel_id=1, source_target_pairs={{0,16},{16,0},{1,17},{17,1},{2,18},{18,2},{3,19},{19,3},{4,20},{20... | collective-permute-start | bytes 1572872 | tf_op jit(solution)/shard_map/ppermute | solution.py:237
  46.3 0.0 collective-permute-done.refs_1_
  46.3 2.4 %collective-permute-start.4 = (bf16[256,1024]{1,0:T(8,128)(2,1)S(1)}, bf16[256,1024]{1,0:T(8,128)(2,1)}, u32[]{:S(2)}, u32[]{:S(2)}) collective-permute-start(bf16[256,1024]{1,0:T(8,128)(2,1)S(1)} %collective-permute-done.refs_1_), channel_id=1, source_target_pairs={{0,16},{16,0},{1,17},{17,1},{2,18},{18,2},{3,19},{19,3},{4,20},{20... | collective-permute-start | bytes 1572872 | tf_op jit(solution)/shard_map/ppermute | solution.py:237
  48.7 0.0 collective-permute-done.1.refs_2_
  48.7 1.9 %collective-permute-start.5 = (bf16[256,1024]{1,0:T(8,128)(2,1)S(1)}, bf16[256,1024]{1,0:T(8,128)(2,1)}, u32[]{:S(2)}, u32[]{:S(2)}) collective-permute-start(bf16[256,1024]{1,0:T(8,128)(2,1)S(1)} %collective-permute-done.1.refs_2_), channel_id=1, source_target_pairs={{0,16},{16,0},{1,17},{17,1},{2,18},{18,2},{3,19},{19,3},{4,20},{20... | collective-permute-start | bytes 1572872 | tf_op jit(solution)/shard_map/ppermute | solution.py:237
  50.6 0.5 all-to-all-done.1.recv_ref
  51.1 0.9 shard_map.70
  52.1 0.0 copy-start.1
  52.1 3.6 %all-to-all-start.2 = ((bf16[4,48,1024]{2,1,0:T(8,128)(2,1)}), bf16[4,48,1024]{2,1,0:T(8,128)(2,1)S(1)}, u32[]{:S(2)}, u32[]{:S(2)}) async-start(bf16[4,48,1024]{2,1,0:T(8,128)(2,1)} %shard_map.70), calls=%async_computation.2 | async-start | bytes 786432 | tf_op jit(solution)/shard_map/all_to_all | solution.py:243
  55.7 0.0 copy-done.1
  55.7 0.6 shard_map.67.base_ref
  56.2 0.0 collective-permute-done.3.refs_4_
  56.3 0.0 copy-start.2
  56.3 0.0 collective-permute-done.6.refs_7_
  56.3 0.0 collective-permute-done.4.refs_5_
  56.3 5.6 %all-to-all-done.2 = bf16[4,48,1024]{2,1,0:T(8,128)(2,1)S(1)} async-done(((bf16[4,48,1024]{2,1,0:T(8,128)(2,1)}), bf16[4,48,1024]{2,1,0:T(8,128)(2,1)S(1)}, u32[]{:S(2)}, u32[]{:S(2)}) %all-to-all-start.2) | async-done | bytes 393248 | tf_op jit(solution)/shard_map/all_to_all | solution.py:243
  61.9 0.0 collective-permute-done.5.refs_6_
  61.9 0.0 copy-done.2
  61.9 3.6 %shard_map.71 = f32[8,32,256]{2,1,0:T(8,128)S(1)} custom-call(f32[2,256]{1,0:T(2,128)S(1)} %shard_map.67.base_ref, bf16[192,1024]{1,0:T(8,128)(2,1)S(1)} %bitcast.12, bf16[256,1024]{1,0:T(8,128)(2,1)S(1)} %copy-done, bf16[256,1024]{1,0:T(8,128)(2,1)S(1)} %collective-permute-done.refs_1_, bf16[256,1024]{1,0:T(8,128)(2,1)S(1)} %collective-permute-done.1.refs_2_, ...), custom_call_target="tpu_custom_call" | custom-call | tf_op jit(solution)/shard_map/pallas_call | solution.py:206
  65.5 16.6 %all_to_all.42.recv_ref = f32[8,32,256]{2,1,0:T(8,128)S(1)} all-to-all(f32[8,32,256]{2,1,0:T(8,128)S(1)} %shard_map.71), channel_id=1, replica_groups=mesh['z'=16,'c'=2,'y'=4,'xa'=1,'xi'=4] {'c','xi'}, dimensions={0} | all-to-all | bytes 524288 | tf_op jit(solution)/shard_map/all_to_all | solution.py:254
  82.1 0.1 shard_map.72
  82.3 6.5 %all_to_all.43 = f32[4,1,128]{2,1,0:T(1,128)S(1)} all-to-all(f32[4,1,128]{2,1,0:T(1,128)S(1)} %bitcast.16), channel_id=1, replica_groups=mesh['z'=16,'c'=2,'y'=4,'xa'=1,'xi'=4] {'y','xa'}, dimensions={0} | all-to-all | bytes 4096 | tf_op jit(solution)/shard_map/all_to_all | solution.py:262
  88.8 19.6 %all_to_all.44 = f32[16,1,128]{2,1,0:T(1,128)S(1)} all-to-all(f32[16,1,128]{2,1,0:T(1,128)S(1)} %bitcast.13), channel_id=1, replica_groups=mesh['z'=16,'c'=2,'y'=4,'xa'=1,'xi'=4] {'z'}, dimensions={0} | all-to-all | bytes 16384 | tf_op jit(solution)/shard_map/all_to_all | solution.py:264
  108.4 0.7 shard_map.74
  (1 shorter events, 0.0 us)
Async XLA Ops:
  2.7 7.7 %copy-start = (bf16[256,1024]{1,0:T(8,128)(2,1)S(1)}, bf16[256,1024]{1,0:T(8,128)(2,1)}, u32[]{:S(2)}) copy-start(bf16[256,1024]{1,0:T(8,128)(2,1)} %refs_0_.1) | copy-start | bytes 1572868
  2.7 16.9 %all-to-all-start = ((bf16[16,16,1024]{2,1,0:T(8,128)(2,1)}), bf16[16,16,1024]{2,1,0:T(8,128)(2,1)S(1)}, u32[]{:S(2)}, u32[]{:S(2)}) async-start(bf16[16,16,1024]{2,1,0:T(8,128)(2,1)} %shard_map.68), calls=%async_computation | async-start | bytes 1048576 | tf_op jit(solution)/shard_map/all_to_all | solution.py:227
  10.5 33.9 %collective-permute-start.2 = (bf16[256,1024]{1,0:T(8,128)(2,1)S(1)}, bf16[256,1024]{1,0:T(8,128)(2,1)S(1)}, u32[]{:S(2)}, u32[]{:S(2)}) collective-permute-start(bf16[256,1024]{1,0:T(8,128)(2,1)S(1)} %copy-done), channel_id=1, source_target_pairs={{3,0},{0,1},{1,2},{2,3},{7,4},{4,5},{5,6},{6,7},{11,8},{8,9},{9,10... | collective-permute-start | bytes 1572872 | tf_op jit(solution)/shard_map/ppermute | solution.py:234
  13.7 32.6 %collective-permute-start = (bf16[256,1024]{1,0:T(8,128)(2,1)S(1)}, bf16[256,1024]{1,0:T(8,128)(2,1)S(1)}, u32[]{:S(2)}, u32[]{:S(2)}) collective-permute-start(bf16[256,1024]{1,0:T(8,128)(2,1)S(1)} %copy-done), channel_id=1, source_target_pairs={{1,0},{2,1},{3,2},{0,3},{5,4},{6,5},{7,6},{4,7},{9,8},{10,9},{11,1... | collective-permute-start | bytes 1572872 | tf_op jit(solution)/shard_map/ppermute | solution.py:234
  20.6 28.1 %collective-permute-start.1 = (bf16[256,1024]{1,0:T(8,128)(2,1)S(1)}, bf16[256,1024]{1,0:T(8,128)(2,1)S(1)}, u32[]{:S(2)}, u32[]{:S(2)}) collective-permute-start(bf16[256,1024]{1,0:T(8,128)(2,1)S(1)} %copy-done), channel_id=1, source_target_pairs={{2,0},{3,1},{0,2},{1,3},{6,4},{7,5},{4,6},{5,7},{10,8},{11,9},{8,1... | collective-permute-start | bytes 1572872 | tf_op jit(solution)/shard_map/ppermute | solution.py:234
  22.9 28.3 %all-to-all-start.1 = ((bf16[16,4,1024]{2,1,0:T(4,128)(2,1)}), bf16[16,4,1024]{2,1,0:T(4,128)(2,1)S(1)}, u32[]{:S(2)}, u32[]{:S(2)}) async-start(bf16[16,4,1024]{2,1,0:T(4,128)(2,1)} %shard_map.69), calls=%async_computation.1 | async-start | bytes 262144 | tf_op jit(solution)/shard_map/all_to_all | solution.py:231
  39.2 17.1 %collective-permute-start.3 = (bf16[256,1024]{1,0:T(8,128)(2,1)S(1)}, bf16[256,1024]{1,0:T(8,128)(2,1)S(1)}, u32[]{:S(2)}, u32[]{:S(2)}) collective-permute-start(bf16[256,1024]{1,0:T(8,128)(2,1)S(1)} %copy-done), channel_id=1, source_target_pairs={{0,16},{16,0},{1,17},{17,1},{2,18},{18,2},{3,19},{19,3},{4,20},{20... | collective-permute-start | bytes 1572872 | tf_op jit(solution)/shard_map/ppermute | solution.py:237
  44.4 11.9 %collective-permute-start.6 = (bf16[256,1024]{1,0:T(8,128)(2,1)S(1)}, bf16[256,1024]{1,0:T(8,128)(2,1)}, u32[]{:S(2)}, u32[]{:S(2)}) collective-permute-start(bf16[256,1024]{1,0:T(8,128)(2,1)S(1)} %collective-permute-done.2.refs_3_), channel_id=1, source_target_pairs={{0,16},{16,0},{1,17},{17,1},{2,18},{18,2},{3,19},{19,3},{4,20},{20... | collective-permute-start | bytes 1572872 | tf_op jit(solution)/shard_map/ppermute | solution.py:237
  46.3 10.0 %collective-permute-start.4 = (bf16[256,1024]{1,0:T(8,128)(2,1)S(1)}, bf16[256,1024]{1,0:T(8,128)(2,1)}, u32[]{:S(2)}, u32[]{:S(2)}) collective-permute-start(bf16[256,1024]{1,0:T(8,128)(2,1)S(1)} %collective-permute-done.refs_1_), channel_id=1, source_target_pairs={{0,16},{16,0},{1,17},{17,1},{2,18},{18,2},{3,19},{19,3},{4,20},{20... | collective-permute-start | bytes 1572872 | tf_op jit(solution)/shard_map/ppermute | solution.py:237
  48.7 13.2 %collective-permute-start.5 = (bf16[256,1024]{1,0:T(8,128)(2,1)S(1)}, bf16[256,1024]{1,0:T(8,128)(2,1)}, u32[]{:S(2)}, u32[]{:S(2)}) collective-permute-start(bf16[256,1024]{1,0:T(8,128)(2,1)S(1)} %collective-permute-done.1.refs_2_), channel_id=1, source_target_pairs={{0,16},{16,0},{1,17},{17,1},{2,18},{18,2},{3,19},{19,3},{4,20},{20... | collective-permute-start | bytes 1572872 | tf_op jit(solution)/shard_map/ppermute | solution.py:237
  52.1 3.6 %copy-start.1 = (bf16[1024]{0:T(1024)(128)(2,1)S(1)}, bf16[1024]{0:T(1024)(128)(2,1)}, u32[]{:S(2)}) copy-start(bf16[1024]{0:T(1024)(128)(2,1)} %center_ref.1) | copy-start | bytes 6148
  52.1 9.8 %all-to-all-start.2 = ((bf16[4,48,1024]{2,1,0:T(8,128)(2,1)}), bf16[4,48,1024]{2,1,0:T(8,128)(2,1)S(1)}, u32[]{:S(2)}, u32[]{:S(2)}) async-start(bf16[4,48,1024]{2,1,0:T(8,128)(2,1)} %shard_map.70), calls=%async_computation.2 | async-start | bytes 786432 | tf_op jit(solution)/shard_map/all_to_all | solution.py:243
  56.3 5.6 %copy-start.2 = (bf16[256,1024]{1,0:T(8,128)(2,1)}, bf16[256,1024]{1,0:T(8,128)(2,1)S(1)}, u32[]{:S(2)}) copy-start(bf16[256,1024]{1,0:T(8,128)(2,1)S(1)} %collective-permute-done.3.refs_4_) | copy-start | bytes 1572868

commit v2 on v1

--- a/solution.py
+++ b/solution.py
@@ -12,10 +12,10 @@
 ROUNDS = 3
 CAP = 4
 ROWS = 131072
-NZ, NC, NY, NXA, NXI = 16, 2, 4, 1, 4
-PLANE = NY * NXA * NXI
-FAR = NY * NXA
-NEAR = NC * NXI
+NZ, NC, NY, NX = 16, 2, 4, 4
+PLANE = NY * NX
+FAR = NC * NY
+NEAR = NX
 BLK = 16
 CNT_ROW = ROUNDS * CAP
 KEEP = ROUNDS * NZ
@@ -65,7 +65,7 @@
 
 
 def compact_kernel(recv_ref, out_ref):
-    place = (lax.axis_index("y") * NXA + lax.axis_index("xa")) * NXI + lax.axis_index("xi")
+    place = lax.axis_index("y") * NX + lax.axis_index("x")
     n = PLANE * BLK
     head = recv_ref[:, 0:128]
     src = iota((n, n), 0)
@@ -117,25 +117,14 @@
 
 
 def near_kernel(base_ref, cands_ref, *refs):
-    here = refs[:NXI]
-    there = refs[NXI:NEAR]
-    out_ref, got_ref, rows_ref, sem = refs[NEAR:]
-    fetches = [pltpu.make_async_copy(src, got_ref.at[k], sem.at[k]) for k, src in enumerate(there)]
-    for fetch in fetches:
-        fetch.start()
+    *pts_refs, out_ref, rows_ref = refs
     cands = cands_ref[...]
     wide = cands.astype(F32)
     norm = jnp.sum(wide * wide, axis=1, keepdims=True)
-    core = lax.axis_index("c")
-    side = lax.axis_index("xi")
-    for k in range(NEAR):
-        block = (core + k // NXI) % NC * NXI + (side + k % NXI) % NXI
-        if k < NXI:
-            pts = here[k][...]
-        else:
-            fetches[k - NXI].wait()
-            pts = got_ref[k - NXI]
-        val = (norm - 2.0 * dot_nt(cands, pts)).reshape(FAR, ROUNDS, NZ, ROWS_DEV)
+    place = lax.axis_index("x")
+    for k, pts_ref in enumerate(pts_refs):
+        block = (place + k) % NEAR
+        val = (norm - 2.0 * dot_nt(cands, pts_ref[...])).reshape(FAR, ROUNDS, NZ, ROWS_DEV)
         least = jnp.min(jnp.min(val, axis=0), axis=1)
         for r in range(ROUNDS):
             rows_ref[pl.ds(r * NEAR + block, 1), :] = least[r : r + 1]
@@ -163,7 +152,7 @@
         sums = jnp.where(lane == r + 1, jnp.sum(running), sums)
     for b in range(NEAR):
         all_ref[b] = running[b : b + 1]
-    run_ref[...] = all_ref[lax.axis_index("c") * NXI + lax.axis_index("xi")]
+    run_ref[...] = all_ref[lax.axis_index("x")]
     sums_ref[...] = sums
 
 
@@ -221,8 +210,8 @@
         ],
     )
     blocks = pack(counts.reshape(ROUNDS), cand_index, points)
-    plane = ("y", "xa", "xi")
-    far = ("y", "xa")
+    plane = ("y", "x")
+    far = ("c", "y")
     blocks, early = lax.optimization_barrier((blocks, points))
     blocks = lax.all_to_all(blocks, plane, 0, 0)
     compact = call(compact_kernel, [vspec()], [((NZ, 4, D), BF16)])
@@ -231,27 +220,19 @@
     mine = lax.all_to_all(mine, "z", 0, 0)
 
     def from_side(rows, k):
-        return lax.ppermute(rows, "xi", [((i + k) % NXI, i) for i in range(NXI)])
-
-    def swap(rows):
-        return lax.ppermute(rows, "c", [(0, 1), (1, 0)])
-
-    here = [points, from_side(early, 1), from_side(shared, 2), from_side(early, 3)]
-    there = [swap(p) for p in here]
+        return lax.ppermute(rows, "x", [((i + k) % NX, i) for i in range(NX)])
+
+    line = [points, from_side(early, 1), from_side(shared, 2), from_side(early, 3)]
     base = call(base_kernel, [vspec()] * 2, [((2, ROWS_DEV), F32)])(points, first_center)
     spread = call(spread_kernel, [vspec()], [((FAR, KEEP, D), BF16)], [VMEM((4 * NZ, D), F32)])
     cands = lax.all_to_all(spread(mine), far, 0, 0).reshape(FAR * KEEP, D)
     near = call(
         near_kernel,
-        [vspec()] * (2 + NXI) + [pl.BlockSpec(memory_space=pl.ANY)] * NXI,
+        [vspec()] * (2 + NEAR),
         [((NEAR, 4 * NEAR, ROWS_DEV), F32)],
-        [
-            VMEM((NXI, ROWS_DEV, D), BF16),
-            VMEM((4 * NEAR, ROWS_DEV), F32),
-            pltpu.SemaphoreType.DMA((NXI,)),
-        ],
-    )
-    mins = lax.all_to_all(near(base, cands, *here, *there), ("c", "xi"), 0, 0)
+        [VMEM((4 * NEAR, ROWS_DEV), F32)],
+    )
+    mins = lax.all_to_all(near(base, cands, *line), "x", 0, 0)
     last = call(
         last_kernel,
         [vspec()],
@@ -272,11 +253,9 @@
 
 
 def solution(mesh):
-    axes = ("z", "c", "y", "xa", "xi")
-    plane = ("y", "xa", "xi")
-    grid = Mesh(mesh.devices.reshape(NZ, NC, NY, NXA, NXI), axes)
-    placed = (P(axes, None), P(), P(None, ("z", "c"), plane), P(None, ("z", "c"), plane, None))
-
+    axes = ("z", "c", "y", "x")
+    grid = Mesh(mesh.devices.reshape(NZ, NC, NY, NX), axes)
+    placed = (P(axes, None), P(), P(None, ("z", "c"), ("y", "x")), P(None, ("z", "c"), ("y", "x"), None))
 
     return jax.shard_map(
         body,

time: 111 us -> 120 us (1.081); the launches traced: 109 us -> 120 us
  blocking collectives: 42.8 us -> 77.1 us
  starting transfers between devices: 47.7 us -> 15.6 us
  waiting for transfers between devices: 8.77 us -> 21.3 us
  Pallas kernels: 8.96 us -> 5.11 us
    all_to_all x1 -> x3, blocking collectives: 16.6 us -> 51.3 us  [the longest x1 27.5 us: body(): mine = lax.all_to_all(mine, 'z', 0, 0)]
    all_to_all x2 -> x0, starting transfers between devices: 24 us -> none  [the longest x1 16.3 us: body(): mine = lax.all_to_all(mine, 'z', 0, 0)]
    ppermute x7 -> x3, waiting for transfers between devices: 0.03 us -> 21.3 us  [from_side(): return lax.ppermute(rows, 'x', [((i + k) % NX, i) for i in range(NX)])]
    ppermute x7 -> x3, starting transfers between devices: 20.1 us -> 8.15 us  [from_side(): return lax.ppermute(rows, 'x', [((i + k) % NX, i) for i in range(NX)])]
    all_to_all x1, waiting for transfers between devices: 5.58 us -> 0.01 us  [body(): cands = lax.all_to_all(spread(mine), far, 0, 0).reshape(FAR * KEEP, D)]
    all_to_all x1, blocking collectives: 19.6 us -> 14.5 us  [body(): sums = lax.all_to_all(relay(sums), 'z', 0, 0)]
    all_to_all x1, blocking collectives: 6.47 us -> 11.2 us  [body(): sums = lax.all_to_all(sums, far, 0, 0)]
    pallas_call x8, Pallas kernels: 8.96 us -> 5.11 us  [run(): return kern(*placed)]
  transfers between devices with their start and end apart: 10 -> 4, of which waited for: 3 -> 2; matrix products, arithmetic and copies ran while one was open for 0% -> 0% of each run, Pallas kernels for 2% -> 0%
where the time goes in v2:
time: 120 us
  blocking collectives  77.1 us (64%)
  waiting for transfers between devices  21.3 us (18%)
  starting transfers between devices  15.6 us (13%)
  Pallas kernels  5.11 us (4%)
    all_to_all x1, blocking collectives, body(): mine = lax.all_to_all(mine, 'z', 0, 0)  27.5 us
    ppermute x3, waiting for transfers between devices, from_side(): return lax.ppermute(rows, 'x', [((i + k) % NX, i) for i in range(NX)])  21.3 us
    all_to_all x1, blocking collectives, body(): blocks = lax.all_to_all(blocks, plane, 0, 0)  17 us
    all_to_all x1, blocking collectives, body(): sums = lax.all_to_all(relay(sums), 'z', 0, 0)  14.5 us
    all_to_all x1, blocking collectives, body(): sums = lax.all_to_all(sums, far, 0, 0)  11.2 us
    ppermute x3, starting transfers between devices, from_side(): return lax.ppermute(rows, 'x', [((i + k) % NX, i) for i in range(NX)])  8.15 us
    all_to_all x1, starting transfers between devices, body(): cands = lax.all_to_all(spread(mine), far, 0, 0).reshape(FAR * KEEP, D)  7.42 us
    all_to_all x1, blocking collectives, body(): mins = lax.all_to_all(near(base, cands, *line), 'x', 0, 0)  6.84 us
  transfers between devices with their start and end apart: 4, of which 2 were waited for; matrix products, arithmetic and copies ran while one was open for 0% of the time, Pallas kernels for 0%

profile of v2, /device:TPU:1, one launch (start us, length us, event | category | flops | bytes accessed | tf_op | source)
XLA Modules:
  0.0 119.8 jit_solution(15275276757418565972)
XLA Ops:
  0.6 1.3 %shard_map.68 = bf16[16,16,1024]{2,1,0:T(8,128)(2,1)S(1)} custom-call(s32[3]{0:T(128)} %bitcast.17, s32[3,1,1,4]{3,2,1,0:T(1,128)} %idx_hbm.1, bf16[256,1024]{1,0:T(8,128)(2,1)} %refs_0_.1), custom_call_target="tpu_custom_call" | custom-call | tf_op jit(solution)/shard_map/pallas_call | solution.py:195
  1.9 17.0 %all_to_all.42 = bf16[16,16,1024]{2,1,0:T(8,128)(2,1)S(1)} all-to-all(bf16[16,16,1024]{2,1,0:T(8,128)(2,1)S(1)} %shard_map.68), channel_id=1, replica_groups=mesh['z'=16,'c'=2,'y'=4,'x'=4] {'y','x'}, dimensions={0} | all-to-all | bytes 1048576 | tf_op jit(solution)/shard_map/all_to_all | solution.py:216
  18.9 0.3 shard_map.69
  19.3 27.5 %all_to_all.43.recv_ref = bf16[16,4,1024]{2,1,0:T(4,128)(2,1)S(1)} all-to-all(bf16[16,4,1024]{2,1,0:T(4,128)(2,1)S(1)} %shard_map.69), channel_id=1, replica_groups=mesh['z'=16,'c'=2,'y'=4,'x'=4] {'z'}, dimensions={0} | all-to-all | bytes 262144 | tf_op jit(solution)/shard_map/all_to_all | solution.py:220
  46.7 1.1 shard_map.70
  47.8 0.0 copy-start
  47.8 0.0 copy-start.1
  47.8 7.4 %all-to-all-start.2 = ((bf16[8,48,1024]{2,1,0:T(8,128)(2,1)}), bf16[8,48,1024]{2,1,0:T(8,128)(2,1)S(1)}, u32[]{:S(2)}, u32[]{:S(2)}) async-start(bf16[8,48,1024]{2,1,0:T(8,128)(2,1)} %shard_map.70), calls=%async_computation.2 | async-start | bytes 1572864 | tf_op jit(solution)/shard_map/all_to_all | solution.py:228
  55.3 0.0 copy-done
  55.3 2.6 %collective-permute-start = (bf16[256,1024]{1,0:T(8,128)(2,1)S(1)}, bf16[256,1024]{1,0:T(8,128)(2,1)S(1)}, u32[]{:S(2)}, u32[]{:S(2)}) collective-permute-start(bf16[256,1024]{1,0:T(8,128)(2,1)S(1)} %copy-done), channel_id=1, source_target_pairs={{1,0},{2,1},{3,2},{0,3},{5,4},{6,5},{7,6},{4,7},{9,8},{10,9},{11,1... | collective-permute-start | bytes 1572872 | tf_op jit(solution)/shard_map/ppermute | solution.py:223
  57.9 2.6 %collective-permute-start.2 = (bf16[256,1024]{1,0:T(8,128)(2,1)S(1)}, bf16[256,1024]{1,0:T(8,128)(2,1)S(1)}, u32[]{:S(2)}, u32[]{:S(2)}) collective-permute-start(bf16[256,1024]{1,0:T(8,128)(2,1)S(1)} %copy-done), channel_id=1, source_target_pairs={{3,0},{0,1},{1,2},{2,3},{7,4},{4,5},{5,6},{6,7},{11,8},{8,9},{9,10... | collective-permute-start | bytes 1572872 | tf_op jit(solution)/shard_map/ppermute | solution.py:223
  60.6 2.9 %collective-permute-start.1 = (bf16[256,1024]{1,0:T(8,128)(2,1)S(1)}, bf16[256,1024]{1,0:T(8,128)(2,1)S(1)}, u32[]{:S(2)}, u32[]{:S(2)}) collective-permute-start(bf16[256,1024]{1,0:T(8,128)(2,1)S(1)} %copy-done), channel_id=1, source_target_pairs={{2,0},{3,1},{0,2},{1,3},{6,4},{7,5},{4,6},{5,7},{10,8},{11,9},{8,1... | collective-permute-start | bytes 1572872 | tf_op jit(solution)/shard_map/ppermute | solution.py:223
  63.4 0.0 copy-done.1
  63.4 0.6 shard_map.67.base_ref
  64.0 6.5 %collective-permute-done.refs_1_ = bf16[256,1024]{1,0:T(8,128)(2,1)S(1)} collective-permute-done((bf16[256,1024]{1,0:T(8,128)(2,1)S(1)}, bf16[256,1024]{1,0:T(8,128)(2,1)S(1)}, u32[]{:S(2)}, u32[]{:S(2)}) %collective-permute-start) | collective-permute-done | bytes 524320 | tf_op jit(solution)/shard_map/ppermute | solution.py:223
  70.5 14.8 %collective-permute-done.2.refs_3_ = bf16[256,1024]{1,0:T(8,128)(2,1)S(1)} collective-permute-done((bf16[256,1024]{1,0:T(8,128)(2,1)S(1)}, bf16[256,1024]{1,0:T(8,128)(2,1)S(1)}, u32[]{:S(2)}, u32[]{:S(2)}) %collective-permute-start.2) | collective-permute-done | bytes 524320 | tf_op jit(solution)/shard_map/ppermute | solution.py:223
  85.3 0.0 collective-permute-done.1.refs_2_
  85.3 0.0 all-to-all-done.2
  85.3 1.1 shard_map.71
  86.4 6.8 %all_to_all.44.recv_ref = f32[4,16,256]{2,1,0:T(8,128)S(1)} all-to-all(f32[4,16,256]{2,1,0:T(8,128)S(1)} %shard_map.71), channel_id=1, replica_groups=mesh['z'=16,'c'=2,'y'=4,'x'=4] {'x'}, dimensions={0} | all-to-all | bytes 131072 | tf_op jit(solution)/shard_map/all_to_all | solution.py:235
  93.2 0.1 shard_map.72
  93.4 11.2 %all_to_all.45 = f32[8,1,128]{2,1,0:T(1,128)S(1)} all-to-all(f32[8,1,128]{2,1,0:T(1,128)S(1)} %bitcast.16), channel_id=1, replica_groups=mesh['z'=16,'c'=2,'y'=4,'x'=4] {'c','y'}, dimensions={0} | all-to-all | bytes 8192 | tf_op jit(solution)/shard_map/all_to_all | solution.py:243
  104.6 14.5 %all_to_all.46 = f32[16,1,128]{2,1,0:T(1,128)S(1)} all-to-all(f32[16,1,128]{2,1,0:T(1,128)S(1)} %bitcast.14), channel_id=1, replica_groups=mesh['z'=16,'c'=2,'y'=4,'x'=4] {'z'}, dimensions={0} | all-to-all | bytes 16384 | tf_op jit(solution)/shard_map/all_to_all | solution.py:245
  119.1 0.7 shard_map.74
  (1 shorter events, 0.0 us)
Async XLA Ops:
  47.8 7.4 %copy-start = (bf16[256,1024]{1,0:T(8,128)(2,1)S(1)}, bf16[256,1024]{1,0:T(8,128)(2,1)}, u32[]{:S(2)}) copy-start(bf16[256,1024]{1,0:T(8,128)(2,1)} %refs_0_.1) | copy-start | bytes 1572868
  47.8 15.6 %copy-start.1 = (bf16[1024]{0:T(1024)(128)(2,1)S(1)}, bf16[1024]{0:T(1024)(128)(2,1)}, u32[]{:S(2)}) copy-start(bf16[1024]{0:T(1024)(128)(2,1)} %center_ref.1) | copy-start | bytes 6148
  47.8 37.5 %all-to-all-start.2 = ((bf16[8,48,1024]{2,1,0:T(8,128)(2,1)}), bf16[8,48,1024]{2,1,0:T(8,128)(2,1)S(1)}, u32[]{:S(2)}, u32[]{:S(2)}) async-start(bf16[8,48,1024]{2,1,0:T(8,128)(2,1)} %shard_map.70), calls=%async_computation.2 | async-start | bytes 1572864 | tf_op jit(solution)/shard_map/all_to_all | solution.py:228
  55.3 15.3 %collective-permute-start = (bf16[256,1024]{1,0:T(8,128)(2,1)S(1)}, bf16[256,1024]{1,0:T(8,128)(2,1)S(1)}, u32[]{:S(2)}, u32[]{:S(2)}) collective-permute-start(bf16[256,1024]{1,0:T(8,128)(2,1)S(1)} %copy-done), channel_id=1, source_target_pairs={{1,0},{2,1},{3,2},{0,3},{5,4},{6,5},{7,6},{4,7},{9,8},{10,9},{11,1... | collective-permute-start | bytes 1572872 | tf_op jit(solution)/shard_map/ppermute | solution.py:223
  57.9 27.4 %collective-permute-start.2 = (bf16[256,1024]{1,0:T(8,128)(2,1)S(1)}, bf16[256,1024]{1,0:T(8,128)(2,1)S(1)}, u32[]{:S(2)}, u32[]{:S(2)}) collective-permute-start(bf16[256,1024]{1,0:T(8,128)(2,1)S(1)} %copy-done), channel_id=1, source_target_pairs={{3,0},{0,1},{1,2},{2,3},{7,4},{4,5},{5,6},{6,7},{11,8},{8,9},{9,10... | collective-permute-start | bytes 1572872 | tf_op jit(solution)/shard_map/ppermute | solution.py:223
  60.6 24.8 %collective-permute-start.1 = (bf16[256,1024]{1,0:T(8,128)(2,1)S(1)}, bf16[256,1024]{1,0:T(8,128)(2,1)S(1)}, u32[]{:S(2)}, u32[]{:S(2)}) collective-permute-start(bf16[256,1024]{1,0:T(8,128)(2,1)S(1)} %copy-done), channel_id=1, source_target_pairs={{2,0},{3,1},{0,2},{1,3},{6,4},{7,5},{4,6},{5,7},{10,8},{11,9},{8,1... | collective-permute-start | bytes 1572872 | tf_op jit(solution)/shard_map/ppermute | solution.py:223

commit v3 on v2

--- a/solution.py
+++ b/solution.py
@@ -14,7 +14,7 @@
 ROWS = 131072
 NZ, NC, NY, NX = 16, 2, 4, 4
 PLANE = NY * NX
-FAR = NC * NY
+FAR = NY
 NEAR = NX
 BLK = 16
 CNT_ROW = ROUNDS * CAP
@@ -116,8 +116,7 @@
     out_ref[1:2] = jnp.maximum(rows_norm + first, 0.0)
 
 
-def near_kernel(base_ref, cands_ref, *refs):
-    *pts_refs, out_ref, rows_ref = refs
+def line_mins(cands_ref, pts_refs, rows_ref):
     cands = cands_ref[...]
     wide = cands.astype(F32)
     norm = jnp.sum(wide * wide, axis=1, keepdims=True)
@@ -128,9 +127,20 @@
         least = jnp.min(jnp.min(val, axis=0), axis=1)
         for r in range(ROUNDS):
             rows_ref[pl.ds(r * NEAR + block, 1), :] = least[r : r + 1]
+
+
+def own_kernel(base_ref, cands_ref, *refs):
+    *pts_refs, rows_ref = refs
     rows_ref[ROUNDS * NEAR : ROUNDS * NEAR + 2, :] = base_ref[...]
     rows_ref[ROUNDS * NEAR + 2 :, :] = jnp.zeros((NEAR - 2, ROWS_DEV), F32)
-    rows = rows_ref[...]
+    line_mins(cands_ref, pts_refs, rows_ref)
+
+
+def other_kernel(own_ref, cands_ref, *refs):
+    *pts_refs, out_ref, rows_ref = refs
+    rows_ref[...] = own_ref[...]
+    line_mins(cands_ref, pts_refs, rows_ref)
+    rows = jnp.minimum(rows_ref[...], own_ref[...])
     for i in range(NEAR):
         out_ref[i] = rows
 
@@ -142,7 +152,7 @@
 
     rows_norm = base_row(0)
     running = base_row(1)
-    lane = iota((FAR, 128), 1)
+    lane = iota((NC * FAR, 128), 1)
     sums = jnp.where(lane == 0, jnp.sum(running), 0.0)
     for r in range(ROUNDS):
         least = recv_ref[0, r * NEAR : (r + 1) * NEAR]
@@ -211,7 +221,6 @@
     )
     blocks = pack(counts.reshape(ROUNDS), cand_index, points)
     plane = ("y", "x")
-    far = ("c", "y")
     blocks, early = lax.optimization_barrier((blocks, points))
     blocks = lax.all_to_all(blocks, plane, 0, 0)
     compact = call(compact_kernel, [vspec()], [((NZ, 4, D), BF16)])
@@ -225,22 +234,20 @@
     line = [points, from_side(early, 1), from_side(shared, 2), from_side(early, 3)]
     base = call(base_kernel, [vspec()] * 2, [((2, ROWS_DEV), F32)])(points, first_center)
     spread = call(spread_kernel, [vspec()], [((FAR, KEEP, D), BF16)], [VMEM((4 * NZ, D), F32)])
-    cands = lax.all_to_all(spread(mine), far, 0, 0).reshape(FAR * KEEP, D)
-    near = call(
-        near_kernel,
-        [vspec()] * (2 + NEAR),
-        [((NEAR, 4 * NEAR, ROWS_DEV), F32)],
-        [VMEM((4 * NEAR, ROWS_DEV), F32)],
-    )
-    mins = lax.all_to_all(near(base, cands, *line), "x", 0, 0)
+    cands = lax.all_to_all(spread(mine), "y", 0, 0).reshape(FAR * KEEP, D)
+    others = lax.ppermute(cands, "c", [(0, 1), (1, 0)])
+    rows = ((4 * NEAR, ROWS_DEV), F32)
+    own = call(own_kernel, [vspec()] * (2 + NEAR), [rows])
+    other = call(other_kernel, [vspec()] * (2 + NEAR), [((NEAR, *rows[0]), F32)], [VMEM(*rows)])
+    mins = lax.all_to_all(other(own(base, cands, *line), others, *line), "x", 0, 0)
     last = call(
         last_kernel,
         [vspec()],
-        [((1, ROWS_DEV), F32), ((FAR, 128), F32)],
+        [((1, ROWS_DEV), F32), ((NC * FAR, 128), F32)],
         [VMEM((NEAR, 1, ROWS_DEV), F32)],
     )
     running, sums = last(mins)
-    sums = lax.all_to_all(sums, far, 0, 0)
+    sums = lax.all_to_all(sums, ("c", "y"), 0, 0)
     relay = call(relay_kernel, [vspec()], [((NZ, 128), F32)])
     sums = lax.all_to_all(relay(sums), "z", 0, 0)
     final = call(

time: 120 us -> 119 us (level)
  waiting for transfers between devices: 21.3 us -> 8.57 us
  blocking collectives: 77.1 us -> 85.2 us
  starting transfers between devices: 15.6 us -> 18.3 us
    ppermute x3, waiting for transfers between devices: 21.3 us -> 8.57 us  [from_side(): return lax.ppermute(rows, 'x', [((i + k) % NX, i) for i in range(NX)])]
    all_to_all x2, blocking collectives: 18.1 us -> 25.2 us  [the longest x1 16.7 us: body(): sums = lax.all_to_all(sums, ('c', 'y'), 0, 0)]
    ppermute x0 -> x1, starting transfers between devices: none -> 6.29 us  [body(): others = lax.ppermute(cands, 'c', [(0, 1), (1, 0)])]
    all_to_all x1, starting transfers between devices: 7.42 us -> 3.59 us  [body(): cands = lax.all_to_all(spread(mine), 'y', 0, 0).reshape(FAR * KEEP, D)]
    pallas_call x8 -> x9, Pallas kernels: 5.11 us -> 5.67 us  [run(): return kern(*placed)]
  transfers between devices with their start and end apart: 4 -> 5, of which waited for: 2 -> 1; matrix products, arithmetic and copies ran while one was open for 0% -> 0% of each run, Pallas kernels for 0% -> 1%
where the time goes in v3:
time: 119 us
  blocking collectives  85.2 us (72%)
  starting transfers between devices  18.3 us (15%)
  waiting for transfers between devices  8.57 us (7%)
  Pallas kernels  5.67 us (5%)
    all_to_all x1, blocking collectives, body(): mine = lax.all_to_all(mine, 'z', 0, 0)  27.5 us
    all_to_all x1, blocking collectives, body(): blocks = lax.all_to_all(blocks, plane, 0, 0)  17 us
    all_to_all x1, blocking collectives, body(): sums = lax.all_to_all(sums, ('c', 'y'), 0, 0)  16.7 us
    all_to_all x1, blocking collectives, body(): sums = lax.all_to_all(relay(sums), 'z', 0, 0)  15.5 us
    ppermute x3, waiting for transfers between devices, from_side(): return lax.ppermute(rows, 'x', [((i + k) % NX, i) for i in range(NX)])  8.57 us
    all_to_all x1, blocking collectives, body(): lax.all_to_all(other(own(base, cands, *line), others, *line), 'x', 0, 0)  8.47 us
    ppermute x3, starting transfers between devices, from_side(): return lax.ppermute(rows, 'x', [((i + k) % NX, i) for i in range(NX)])  8.41 us
    ppermute x1, starting transfers between devices, body(): others = lax.ppermute(cands, 'c', [(0, 1), (1, 0)])  6.29 us
  transfers between devices with their start and end apart: 5, of which 1 were waited for; matrix products, arithmetic and copies ran while one was open for 0% of the time, Pallas kernels for 1%

profile of v3, /device:TPU:1, one launch (start us, length us, event | category | flops | bytes accessed | tf_op | source)
XLA Modules:
  0.0 118.5 jit_solution(1599143647586043239)
XLA Ops:
  0.6 1.3 %shard_map.68 = bf16[16,16,1024]{2,1,0:T(8,128)(2,1)S(1)} custom-call(s32[3]{0:T(128)} %bitcast.18, s32[3,1,1,4]{3,2,1,0:T(1,128)} %idx_hbm.1, bf16[256,1024]{1,0:T(8,128)(2,1)} %refs_0_.3), custom_call_target="tpu_custom_call" | custom-call | tf_op jit(solution)/shard_map/pallas_call | solution.py:205
  1.9 17.0 %all_to_all.42 = bf16[16,16,1024]{2,1,0:T(8,128)(2,1)S(1)} all-to-all(bf16[16,16,1024]{2,1,0:T(8,128)(2,1)S(1)} %shard_map.68), channel_id=1, replica_groups=mesh['z'=16,'c'=2,'y'=4,'x'=4] {'y','x'}, dimensions={0} | all-to-all | bytes 1048576 | tf_op jit(solution)/shard_map/all_to_all | solution.py:225
  18.9 0.3 shard_map.69
  19.3 27.5 %all_to_all.43.recv_ref = bf16[16,4,1024]{2,1,0:T(4,128)(2,1)S(1)} all-to-all(bf16[16,4,1024]{2,1,0:T(4,128)(2,1)S(1)} %shard_map.69), channel_id=1, replica_groups=mesh['z'=16,'c'=2,'y'=4,'x'=4] {'z'}, dimensions={0} | all-to-all | bytes 262144 | tf_op jit(solution)/shard_map/all_to_all | solution.py:229
  46.7 0.9 shard_map.70
  47.7 0.0 copy-start
  47.7 0.0 copy-start.1
  47.7 3.6 %all-to-all-start.2 = ((bf16[4,48,1024]{2,1,0:T(8,128)(2,1)}), bf16[4,48,1024]{2,1,0:T(8,128)(2,1)S(1)}, u32[]{:S(2)}, u32[]{:S(2)}) async-start(bf16[4,48,1024]{2,1,0:T(8,128)(2,1)} %shard_map.70), calls=%async_computation.2 | async-start | bytes 786432 | tf_op jit(solution)/shard_map/all_to_all | solution.py:237
  51.3 0.0 copy-done
  51.3 2.2 %collective-permute-start.2 = (bf16[256,1024]{1,0:T(8,128)(2,1)S(1)}, bf16[256,1024]{1,0:T(8,128)(2,1)S(1)}, u32[]{:S(2)}, u32[]{:S(2)}) collective-permute-start(bf16[256,1024]{1,0:T(8,128)(2,1)S(1)} %copy-done), channel_id=1, source_target_pairs={{3,0},{0,1},{1,2},{2,3},{7,4},{4,5},{5,6},{6,7},{11,8},{8,9},{9,10... | collective-permute-start | bytes 1572872 | tf_op jit(solution)/shard_map/ppermute | solution.py:232
  53.5 4.3 %collective-permute-start = (bf16[256,1024]{1,0:T(8,128)(2,1)S(1)}, bf16[256,1024]{1,0:T(8,128)(2,1)S(1)}, u32[]{:S(2)}, u32[]{:S(2)}) collective-permute-start(bf16[256,1024]{1,0:T(8,128)(2,1)S(1)} %copy-done), channel_id=1, source_target_pairs={{1,0},{2,1},{3,2},{0,3},{5,4},{6,5},{7,6},{4,7},{9,8},{10,9},{11,1... | collective-permute-start | bytes 1572872 | tf_op jit(solution)/shard_map/ppermute | solution.py:232
  57.8 1.9 %collective-permute-start.1 = (bf16[256,1024]{1,0:T(8,128)(2,1)S(1)}, bf16[256,1024]{1,0:T(8,128)(2,1)S(1)}, u32[]{:S(2)}, u32[]{:S(2)}) collective-permute-start(bf16[256,1024]{1,0:T(8,128)(2,1)S(1)} %copy-done), channel_id=1, source_target_pairs={{2,0},{3,1},{0,2},{1,3},{6,4},{7,5},{4,6},{5,7},{10,8},{11,9},{8,1... | collective-permute-start | bytes 1572872 | tf_op jit(solution)/shard_map/ppermute | solution.py:232
  59.7 0.0 all-to-all-done.2
  59.7 6.3 %collective-permute-start.3 = (bf16[192,1024]{1,0:T(8,128)(2,1)S(1)}, bf16[192,1024]{1,0:T(8,128)(2,1)S(1)}, u32[]{:S(2)}, u32[]{:S(2)}) collective-permute-start(bf16[192,1024]{1,0:T(8,128)(2,1)S(1)} %bitcast.12), channel_id=1, source_target_pairs={{0,16},{16,0},{1,17},{17,1},{2,18},{18,2},{3,19},{19,3},{4,20},{20... | collective-permute-start | bytes 1179656 | tf_op jit(solution)/shard_map/ppermute | solution.py:238
  66.0 0.0 copy-done.1
  66.0 0.6 shard_map.67.base_ref
  66.6 0.0 collective-permute-done.2.refs_3_
  66.6 0.0 collective-permute-done.refs_1_
  66.6 8.6 %collective-permute-done.1.refs_2_ = bf16[256,1024]{1,0:T(8,128)(2,1)S(1)} collective-permute-done((bf16[256,1024]{1,0:T(8,128)(2,1)S(1)}, bf16[256,1024]{1,0:T(8,128)(2,1)S(1)}, u32[]{:S(2)}, u32[]{:S(2)}) %collective-permute-start.1) | collective-permute-done | bytes 524320 | tf_op jit(solution)/shard_map/ppermute | solution.py:232
  75.2 0.9 shard_map.71.own_ref
  76.1 0.0 collective-permute-done.3.cands_ref
  76.1 0.9 shard_map.72
  77.0 8.5 %all_to_all.44.recv_ref = f32[4,16,256]{2,1,0:T(8,128)S(1)} all-to-all(f32[4,16,256]{2,1,0:T(8,128)S(1)} %shard_map.72), channel_id=1, replica_groups=mesh['z'=16,'c'=2,'y'=4,'x'=4] {'x'}, dimensions={0} | all-to-all | bytes 131072 | tf_op jit(solution)/shard_map/all_to_all | solution.py:242
  85.4 0.1 shard_map.73
  85.6 16.7 %all_to_all.45 = f32[8,1,128]{2,1,0:T(1,128)S(1)} all-to-all(f32[8,1,128]{2,1,0:T(1,128)S(1)} %bitcast.17), channel_id=1, replica_groups=mesh['z'=16,'c'=2,'y'=4,'x'=4] {'c','y'}, dimensions={0} | all-to-all | bytes 8192 | tf_op jit(solution)/shard_map/all_to_all | solution.py:250
  102.3 15.5 %all_to_all.46 = f32[16,1,128]{2,1,0:T(1,128)S(1)} all-to-all(f32[16,1,128]{2,1,0:T(1,128)S(1)} %bitcast.15), channel_id=1, replica_groups=mesh['z'=16,'c'=2,'y'=4,'x'=4] {'z'}, dimensions={0} | all-to-all | bytes 16384 | tf_op jit(solution)/shard_map/all_to_all | solution.py:252
  117.9 0.7 shard_map.75
  (1 shorter events, 0.0 us)
Async XLA Ops:
  47.7 3.6 %copy-start = (bf16[256,1024]{1,0:T(8,128)(2,1)S(1)}, bf16[256,1024]{1,0:T(8,128)(2,1)}, u32[]{:S(2)}) copy-start(bf16[256,1024]{1,0:T(8,128)(2,1)} %refs_0_.3) | copy-start | bytes 1572868
  47.7 18.4 %copy-start.1 = (bf16[1024]{0:T(1024)(128)(2,1)S(1)}, bf16[1024]{0:T(1024)(128)(2,1)}, u32[]{:S(2)}) copy-start(bf16[1024]{0:T(1024)(128)(2,1)} %center_ref.1) | copy-start | bytes 6148
  47.7 12.0 %all-to-all-start.2 = ((bf16[4,48,1024]{2,1,0:T(8,128)(2,1)}), bf16[4,48,1024]{2,1,0:T(8,128)(2,1)S(1)}, u32[]{:S(2)}, u32[]{:S(2)}) async-start(bf16[4,48,1024]{2,1,0:T(8,128)(2,1)} %shard_map.70), calls=%async_computation.2 | async-start | bytes 786432 | tf_op jit(solution)/shard_map/all_to_all | solution.py:237
  51.3 15.3 %collective-permute-start.2 = (bf16[256,1024]{1,0:T(8,128)(2,1)S(1)}, bf16[256,1024]{1,0:T(8,128)(2,1)S(1)}, u32[]{:S(2)}, u32[]{:S(2)}) collective-permute-start(bf16[256,1024]{1,0:T(8,128)(2,1)S(1)} %copy-done), channel_id=1, source_target_pairs={{3,0},{0,1},{1,2},{2,3},{7,4},{4,5},{5,6},{6,7},{11,8},{8,9},{9,10... | collective-permute-start | bytes 1572872 | tf_op jit(solution)/shard_map/ppermute | solution.py:232
  53.5 13.1 %collective-permute-start = (bf16[256,1024]{1,0:T(8,128)(2,1)S(1)}, bf16[256,1024]{1,0:T(8,128)(2,1)S(1)}, u32[]{:S(2)}, u32[]{:S(2)}) collective-permute-start(bf16[256,1024]{1,0:T(8,128)(2,1)S(1)} %copy-done), channel_id=1, source_target_pairs={{1,0},{2,1},{3,2},{0,3},{5,4},{6,5},{7,6},{4,7},{9,8},{10,9},{11,1... | collective-permute-start | bytes 1572872 | tf_op jit(solution)/shard_map/ppermute | solution.py:232
  57.8 17.4 %collective-permute-start.1 = (bf16[256,1024]{1,0:T(8,128)(2,1)S(1)}, bf16[256,1024]{1,0:T(8,128)(2,1)S(1)}, u32[]{:S(2)}, u32[]{:S(2)}) collective-permute-start(bf16[256,1024]{1,0:T(8,128)(2,1)S(1)} %copy-done), channel_id=1, source_target_pairs={{2,0},{3,1},{0,2},{1,3},{6,4},{7,5},{4,6},{5,7},{10,8},{11,9},{8,1... | collective-permute-start | bytes 1572872 | tf_op jit(solution)/shard_map/ppermute | solution.py:232
  59.7 16.3 %collective-permute-start.3 = (bf16[192,1024]{1,0:T(8,128)(2,1)S(1)}, bf16[192,1024]{1,0:T(8,128)(2,1)S(1)}, u32[]{:S(2)}, u32[]{:S(2)}) collective-permute-start(bf16[192,1024]{1,0:T(8,128)(2,1)S(1)} %bitcast.12), channel_id=1, source_target_pairs={{0,16},{16,0},{1,17},{17,1},{2,18},{18,2},{3,19},{19,3},{4,20},{20... | collective-permute-start | bytes 1179656 | tf_op jit(solution)/shard_map/ppermute | solution.py:238

commit v4 on v3

--- a/solution.py
+++ b/solution.py
@@ -16,8 +16,9 @@
 PLANE = NY * NX
 FAR = NY
 NEAR = NX
-BLK = 16
-CNT_ROW = ROUNDS * CAP
+SLOTS = ROUNDS * CAP
+LANES = 128
+FOLD = D // LANES
 KEEP = ROUNDS * NZ
 
 VMEM = pltpu.VMEM
@@ -47,57 +48,71 @@
     fetch.start()
     fetch_idx.wait()
     fetch_cnt.wait()
-    sub = iota((BLK, ROWS_DEV), 0)
-    lane = iota((BLK, ROWS_DEV), 1)
-    want = jnp.full((BLK, ROWS_DEV), -1, jnp.int32)
-    for q in range(CNT_ROW):
-        want = jnp.where(sub == q, idx_ref[q // CAP, 0, 0, q % CAP], want)
+    sub = iota((16, ROWS_DEV), 0)
+    lane = iota((16, ROWS_DEV), 1)
+    want = jnp.full((16, ROWS_DEV), -1, jnp.int32)
+    for q in range(SLOTS):
+        r, j = divmod(q, CAP)
+        row = jnp.where(j < cnt_ref[r], idx_ref[r, 0, 0, j], -1)
+        want = jnp.where(sub == q, row, want)
     fetch.wait()
     rows = jnp.dot(one_hot(lane == want), pts_ref[...], preferred_element_type=F32)
-    sub = iota((BLK, D), 0)
-    lane = iota((BLK, D), 1)
-    for r in range(ROUNDS):
-        here = jnp.logical_and(sub == CNT_ROW, lane == r)
-        rows = jnp.where(here, cnt_ref[r].astype(F32), rows)
-    rows = rows.astype(BF16)
+    dead = jnp.logical_and(want < 0, lane == 0)[:, :LANES]
+    head = jnp.where(dead, jnp.inf, rows[:, :LANES]).astype(BF16)
+    tail = rows[:, LANES:].astype(BF16)
     for i in range(PLANE):
-        out_ref[i] = rows
-
-
-def compact_kernel(recv_ref, out_ref):
+        for r in range(ROUNDS):
+            out_ref[i, r, :, :LANES] = head[r * CAP : (r + 1) * CAP]
+            out_ref[i, r, :, LANES:] = tail[r * CAP : (r + 1) * CAP]
+
+
+def compact_kernel(recv_ref, out_ref, tmp_ref, fold_ref):
     place = lax.axis_index("y") * NX + lax.axis_index("x")
-    n = PLANE * BLK
-    head = recv_ref[:, 0:128]
+    n = PLANE * SLOTS
+    for s in range(PLANE):
+        for r in range(ROUNDS):
+            at = s * SLOTS + r * CAP
+            tmp_ref[at : at + CAP, :] = recv_ref[s, r].astype(F32)
+    head = tmp_ref[:, :LANES]
+    dead = head == jnp.inf
+    live = one_hot(jnp.logical_not(dead))
     src = iota((n, n), 0)
     dst = iota((n, n), 1)
-    is_cnt = src % BLK == CNT_ROW
-    own = one_hot(jnp.logical_and(is_cnt, src // BLK == dst // BLK))
-    before = one_hot(jnp.logical_and(is_cnt, src // BLK < dst // BLK))
+    same = src % SLOTS // CAP == dst % SLOTS // CAP
+    before = one_hot(jnp.logical_and(same, src < dst))
+    here = one_hot(src == dst)
     contract = (((0,), (0,)), ((), ()))
-    cnt = lax.dot_general(head, own, contract, preferred_element_type=F32)[:16]
-    off = lax.dot_general(head, before, contract, preferred_element_type=F32)[:16]
-    r = iota((16, n), 0)
-    q = iota((16, n), 1) % BLK
-    j = (q % CAP).astype(F32)
-    live = jnp.logical_and(q < CNT_ROW, q // CAP == r)
-    live = jnp.logical_and(live, j < cnt)
-    live = jnp.logical_and(live, off + j == place.astype(F32))
-    rows = jnp.dot(one_hot(live), recv_ref[...], preferred_element_type=F32)
-    rows = rows[0:4].astype(BF16)
+    pos = lax.dot_general(live, before, contract, preferred_element_type=F32)[0:1]
+    alive = lax.dot_general(live, here, contract, preferred_element_type=F32)[0:1]
+    slot = jnp.where(alive > 0.5, pos, -1.0)
+    round_of = iota((16, n), 1) % SLOTS // CAP
+    take = jnp.logical_and(round_of == iota((16, n), 0), slot == place.astype(F32))
+    take = one_hot(take)
+    head = jnp.where(dead, 0.0, head).astype(BF16)
+    head = jnp.dot(take, head, preferred_element_type=F32)
+    tail = jnp.dot(take, tmp_ref[:, LANES:].astype(BF16), preferred_element_type=F32)
+    rows = jnp.concatenate([head, tail], axis=1)
+    for r in range(ROUNDS):
+        for f in range(FOLD):
+            at = r * FOLD + f
+            fold_ref[at : at + 1, :] = rows[r : r + 1, f * LANES : (f + 1) * LANES]
+    block = fold_ref[...].astype(BF16)
     for i in range(NZ):
-        out_ref[i] = rows
-
-
-def spread_kernel(recv_ref, out_ref, tmp_ref):
-    for z in range(NZ):
-        tmp_ref[4 * z : 4 * z + 4, :] = recv_ref[z].astype(F32)
-    m = iota((KEEP, 4 * NZ), 0)
-    k = iota((KEEP, 4 * NZ), 1)
-    sel = one_hot(k == 4 * (m % NZ) + m // NZ)
-    rows = jnp.dot(sel, tmp_ref[...].astype(BF16), preferred_element_type=F32)
-    rows = rows.astype(BF16)
+        out_ref[i] = block
+
+
+def spread_kernel(recv_ref, out_ref):
+    n = NZ * ROUNDS * FOLD
+    m = iota((n, n), 0)
+    k = iota((n, n), 1)
+    z = m % NZ
+    r = m // NZ % ROUNDS
+    f = m // KEEP
+    sel = one_hot(k == (z * ROUNDS + r) * FOLD + f)
+    parts = jnp.dot(sel, recv_ref[...], preferred_element_type=F32).astype(BF16)
     for i in range(FAR):
-        out_ref[i] = rows
+        for f in range(FOLD):
+            out_ref[i, :, f * LANES : (f + 1) * LANES] = parts[f * KEEP : (f + 1) * KEEP]
 
 
 def base_kernel(pts_ref, center_ref, out_ref):
@@ -211,7 +226,7 @@
     pack = call(
         pack_kernel,
         [pl.BlockSpec(memory_space=pl.ANY)] * 3,
-        [((PLANE, BLK, D), BF16)],
+        [((PLANE, ROUNDS, CAP, D), BF16)],
         [
             SMEM((ROUNDS,), jnp.int32),
             SMEM((ROUNDS, 1, 1, CAP), jnp.int32),
@@ -223,17 +238,24 @@
     plane = ("y", "x")
     blocks, early = lax.optimization_barrier((blocks, points))
     blocks = lax.all_to_all(blocks, plane, 0, 0)
-    compact = call(compact_kernel, [vspec()], [((NZ, 4, D), BF16)])
-    mine = compact(blocks.reshape(PLANE * BLK, D))
-    mine, shared = lax.optimization_barrier((mine, points))
+    compact = call(
+        compact_kernel,
+        [vspec()],
+        [((NZ, ROUNDS * FOLD, LANES), BF16)],
+        [VMEM((PLANE * SLOTS, D), F32), VMEM((ROUNDS * FOLD, LANES), F32)],
+    )
+    mine = compact(blocks)
     mine = lax.all_to_all(mine, "z", 0, 0)
 
     def from_side(rows, k):
         return lax.ppermute(rows, "x", [((i + k) % NX, i) for i in range(NX)])
 
-    line = [points, from_side(early, 1), from_side(shared, 2), from_side(early, 3)]
+    right = from_side(early, 1)
+    far_side = lax.ppermute(right, "x", [((i + 1) % NX, i) for i in range(NX)])
+    line = [points, right, far_side, from_side(early, 3)]
     base = call(base_kernel, [vspec()] * 2, [((2, ROWS_DEV), F32)])(points, first_center)
-    spread = call(spread_kernel, [vspec()], [((FAR, KEEP, D), BF16)], [VMEM((4 * NZ, D), F32)])
+    spread = call(spread_kernel, [vspec()], [((FAR, KEEP, D), BF16)])
+    mine = mine.reshape(NZ * ROUNDS * FOLD, LANES)
     cands = lax.all_to_all(spread(mine), "y", 0, 0).reshape(FAR * KEEP, D)
     others = lax.ppermute(cands, "c", [(0, 1), (1, 0)])
     rows = ((4 * NEAR, ROWS_DEV), F32)

time: 119 us -> 107 us (0.90)
  blocking collectives: 85.2 us -> 54 us
  starting transfers between devices: 18.3 us -> 34.1 us
  waiting for transfers between devices: 8.57 us -> 10.6 us
    all_to_all x1 -> x0, blocking collectives: 27.5 us -> none  [body(): mine = lax.all_to_all(mine, 'z', 0, 0)]
    all_to_all x0 -> x1, starting transfers between devices: none -> 15.7 us  [body(): mine = lax.all_to_all(mine, 'z', 0, 0)]
    all_to_all x0 -> x1, waiting for transfers between devices: none -> 9.39 us  [body(): mine = lax.all_to_all(mine, 'z', 0, 0)]
    ppermute x3 -> x2, waiting for transfers between devices: 8.57 us -> 0.33 us  [from_side(): return lax.ppermute(rows, 'x', [((i + k) % NX, i) for i in range(NX)])]
    ppermute x0 -> x1, starting transfers between devices: none -> 4.33 us  [body(): far_side = lax.ppermute(right, 'x', [((i + 1) % NX, i) for i in range(NX)])]
    ppermute x3 -> x2, starting transfers between devices: 8.41 us -> 4.6 us  [from_side(): return lax.ppermute(rows, 'x', [((i + k) % NX, i) for i in range(NX)])]
    all_to_all x1, blocking collectives: 16.7 us -> 14.7 us  [body(): sums = lax.all_to_all(sums, ('c', 'y'), 0, 0)]
  transfers between devices with their start and end apart: 5 -> 6, of which waited for: 1 -> 3; matrix products, arithmetic and copies ran while one was open for 0% -> 0% of each run, Pallas kernels for 1% -> 2%
where the time goes in v4:
time: 107 us; the launch traced here: 106 us
  blocking collectives  54 us (50%)
  starting transfers between devices  34.1 us (32%)
  waiting for transfers between devices  10.6 us (10%)
  Pallas kernels  6.6 us (6%)
    all_to_all x1, blocking collectives, body(): blocks = lax.all_to_all(blocks, plane, 0, 0)  15.9 us
    all_to_all x1, starting transfers between devices, body(): mine = lax.all_to_all(mine, 'z', 0, 0)  15.7 us
    all_to_all x1, blocking collectives, body(): sums = lax.all_to_all(sums, ('c', 'y'), 0, 0)  14.7 us
    all_to_all x1, blocking collectives, body(): sums = lax.all_to_all(relay(sums), 'z', 0, 0)  14.6 us
    all_to_all x1, waiting for transfers between devices, body(): mine = lax.all_to_all(mine, 'z', 0, 0)  9.39 us
    all_to_all x1, blocking collectives, body(): lax.all_to_all(other(own(base, cands, *line), others, *line), 'x', 0, 0)  8.95 us
    pallas_call x9, Pallas kernels, run(): return kern(*placed)  6.6 us
    ppermute x1, starting transfers between devices, body(): others = lax.ppermute(cands, 'c', [(0, 1), (1, 0)])  5.93 us
  transfers between devices with their start and end apart: 6, of which 3 were waited for; matrix products, arithmetic and copies ran while one was open for 0% of the time, Pallas kernels for 2%

profile of v4, /device:TPU:1, one launch (start us, length us, event | category | flops | bytes accessed | tf_op | source)
XLA Modules:
  0.0 106.2 jit_solution(15706768066717525228)
XLA Ops:
  0.6 1.3 %shard_map.68 = bf16[16,3,4,1024]{3,2,1,0:T(4,128)(2,1)S(1)} custom-call(s32[3]{0:T(128)} %bitcast.18, s32[3,1,1,4]{3,2,1,0:T(1,128)} %idx_hbm.1, bf16[256,1024]{1,0:T(8,128)(2,1)} %refs_0_.3), custom_call_target="tpu_custom_call" | custom-call | tf_op jit(solution)/shard_map/pallas_call | solution.py:220
  1.9 15.9 %all_to_all.42.recv_ref = bf16[16,3,4,1024]{3,2,1,0:T(4,128)(2,1)S(1)} all-to-all(bf16[16,3,4,1024]{3,2,1,0:T(4,128)(2,1)S(1)} %shard_map.68), channel_id=1, replica_groups=mesh['z'=16,'c'=2,'y'=4,'x'=4] {'y','x'}, dimensions={0} | all-to-all | bytes 786432 | tf_op jit(solution)/shard_map/all_to_all | solution.py:240
  17.8 0.0 copy-start
  17.8 1.1 %shard_map.69 = bf16[16,24,128]{2,1,0:T(8,128)(2,1)} custom-call(bf16[16,3,4,1024]{3,2,1,0:T(4,128)(2,1)S(1)} %all_to_all.42.recv_ref), custom_call_target="tpu_custom_call" | custom-call | tf_op jit(solution)/shard_map/pallas_call | solution.py:220
  18.9 15.7 %all-to-all-start.1 = ((bf16[16,24,128]{2,1,0:T(8,128)(2,1)}), bf16[16,24,128]{2,1,0:T(8,128)(2,1)S(1)}, u32[]{:S(2)}, u32[]{:S(2)}) async-start(bf16[16,24,128]{2,1,0:T(8,128)(2,1)} %shard_map.69), calls=%async_computation.1 | async-start | bytes 196608 | tf_op jit(solution)/shard_map/all_to_all | solution.py:248
  34.6 0.0 copy-done
  34.6 2.4 %collective-permute-start = (bf16[256,1024]{1,0:T(8,128)(2,1)S(1)}, bf16[256,1024]{1,0:T(8,128)(2,1)S(1)}, u32[]{:S(2)}, u32[]{:S(2)}) collective-permute-start(bf16[256,1024]{1,0:T(8,128)(2,1)S(1)} %copy-done), channel_id=1, source_target_pairs={{1,0},{2,1},{3,2},{0,3},{5,4},{6,5},{7,6},{4,7},{9,8},{10,9},{11,1... | collective-permute-start | bytes 1572872 | tf_op jit(solution)/shard_map/ppermute | solution.py:251
  37.0 9.4 %all-to-all-done.1 = bf16[16,24,128]{2,1,0:T(8,128)(2,1)S(1)} async-done(((bf16[16,24,128]{2,1,0:T(8,128)(2,1)}), bf16[16,24,128]{2,1,0:T(8,128)(2,1)S(1)}, u32[]{:S(2)}, u32[]{:S(2)}) %all-to-all-start.1) | async-done | bytes 98336 | tf_op jit(solution)/shard_map/all_to_all | solution.py:248
  46.4 1.1 shard_map.70
  47.5 0.0 copy-start.1
  47.5 3.6 %all-to-all-start.2 = ((bf16[4,48,1024]{2,1,0:T(8,128)(2,1)}), bf16[4,48,1024]{2,1,0:T(8,128)(2,1)S(1)}, u32[]{:S(2)}, u32[]{:S(2)}) async-start(bf16[4,48,1024]{2,1,0:T(8,128)(2,1)} %shard_map.70), calls=%async_computation.2 | async-start | bytes 786432 | tf_op jit(solution)/shard_map/all_to_all | solution.py:259
  51.1 2.2 %collective-permute-start.2 = (bf16[256,1024]{1,0:T(8,128)(2,1)S(1)}, bf16[256,1024]{1,0:T(8,128)(2,1)S(1)}, u32[]{:S(2)}, u32[]{:S(2)}) collective-permute-start(bf16[256,1024]{1,0:T(8,128)(2,1)S(1)} %copy-done), channel_id=1, source_target_pairs={{3,0},{0,1},{1,2},{2,3},{7,4},{4,5},{5,6},{6,7},{11,8},{8,9},{9,10... | collective-permute-start | bytes 1572872 | tf_op jit(solution)/shard_map/ppermute | solution.py:251
  53.3 0.0 collective-permute-done.refs_1_
  53.3 4.3 %collective-permute-start.1 = (bf16[256,1024]{1,0:T(8,128)(2,1)S(1)}, bf16[256,1024]{1,0:T(8,128)(2,1)S(1)}, u32[]{:S(2)}, u32[]{:S(2)}) collective-permute-start(bf16[256,1024]{1,0:T(8,128)(2,1)S(1)} %collective-permute-done.refs_1_), channel_id=1, source_target_pairs={{1,0},{2,1},{3,2},{0,3},{5,4},{6,5},{7,6},{4,7},{9,8},{10,9},{11,1... | collective-permute-start | bytes 1572872 | tf_op jit(solution)/shard_map/ppermute | solution.py:254
  57.6 0.0 all-to-all-done.2
  57.6 5.9 %collective-permute-start.3 = (bf16[192,1024]{1,0:T(8,128)(2,1)S(1)}, bf16[192,1024]{1,0:T(8,128)(2,1)S(1)}, u32[]{:S(2)}, u32[]{:S(2)}) collective-permute-start(bf16[192,1024]{1,0:T(8,128)(2,1)S(1)} %bitcast.11), channel_id=1, source_target_pairs={{0,16},{16,0},{1,17},{17,1},{2,18},{18,2},{3,19},{19,3},{4,20},{20... | collective-permute-start | bytes 1179656 | tf_op jit(solution)/shard_map/ppermute | solution.py:260
  63.6 0.0 copy-done.1
  63.6 0.6 shard_map.67.base_ref
  64.1 0.3 collective-permute-done.2.refs_3_
  64.4 0.9 collective-permute-done.1.refs_2_
  65.4 0.9 shard_map.71.own_ref
  66.2 0.0 collective-permute-done.3.cands_ref
  66.3 0.9 shard_map.72
  67.2 9.0 %all_to_all.43.recv_ref = f32[4,16,256]{2,1,0:T(8,128)S(1)} all-to-all(f32[4,16,256]{2,1,0:T(8,128)S(1)} %shard_map.72), channel_id=1, replica_groups=mesh['z'=16,'c'=2,'y'=4,'x'=4] {'x'}, dimensions={0} | all-to-all | bytes 131072 | tf_op jit(solution)/shard_map/all_to_all | solution.py:264
  76.1 0.1 shard_map.73
  76.3 14.7 %all_to_all.44 = f32[8,1,128]{2,1,0:T(1,128)S(1)} all-to-all(f32[8,1,128]{2,1,0:T(1,128)S(1)} %bitcast.17), channel_id=1, replica_groups=mesh['z'=16,'c'=2,'y'=4,'x'=4] {'c','y'}, dimensions={0} | all-to-all | bytes 8192 | tf_op jit(solution)/shard_map/all_to_all | solution.py:272
  90.9 14.6 %all_to_all.45 = f32[16,1,128]{2,1,0:T(1,128)S(1)} all-to-all(f32[16,1,128]{2,1,0:T(1,128)S(1)} %bitcast.15), channel_id=1, replica_groups=mesh['z'=16,'c'=2,'y'=4,'x'=4] {'z'}, dimensions={0} | all-to-all | bytes 16384 | tf_op jit(solution)/shard_map/all_to_all | solution.py:274
  105.5 0.7 shard_map.75
  (1 shorter events, 0.0 us)
Async XLA Ops:
  17.8 16.8 %copy-start = (bf16[256,1024]{1,0:T(8,128)(2,1)S(1)}, bf16[256,1024]{1,0:T(8,128)(2,1)}, u32[]{:S(2)}) copy-start(bf16[256,1024]{1,0:T(8,128)(2,1)} %refs_0_.3) | copy-start | bytes 1572868
  18.9 27.5 %all-to-all-start.1 = ((bf16[16,24,128]{2,1,0:T(8,128)(2,1)}), bf16[16,24,128]{2,1,0:T(8,128)(2,1)S(1)}, u32[]{:S(2)}, u32[]{:S(2)}) async-start(bf16[16,24,128]{2,1,0:T(8,128)(2,1)} %shard_map.69), calls=%async_computation.1 | async-start | bytes 196608 | tf_op jit(solution)/shard_map/all_to_all | solution.py:248
  34.6 18.7 %collective-permute-start = (bf16[256,1024]{1,0:T(8,128)(2,1)S(1)}, bf16[256,1024]{1,0:T(8,128)(2,1)S(1)}, u32[]{:S(2)}, u32[]{:S(2)}) collective-permute-start(bf16[256,1024]{1,0:T(8,128)(2,1)S(1)} %copy-done), channel_id=1, source_target_pairs={{1,0},{2,1},{3,2},{0,3},{5,4},{6,5},{7,6},{4,7},{9,8},{10,9},{11,1... | collective-permute-start | bytes 1572872 | tf_op jit(solution)/shard_map/ppermute | solution.py:251
  47.5 16.1 %copy-start.1 = (bf16[1024]{0:T(1024)(128)(2,1)S(1)}, bf16[1024]{0:T(1024)(128)(2,1)}, u32[]{:S(2)}) copy-start(bf16[1024]{0:T(1024)(128)(2,1)} %center_ref.1) | copy-start | bytes 6148
  47.5 10.1 %all-to-all-start.2 = ((bf16[4,48,1024]{2,1,0:T(8,128)(2,1)}), bf16[4,48,1024]{2,1,0:T(8,128)(2,1)S(1)}, u32[]{:S(2)}, u32[]{:S(2)}) async-start(bf16[4,48,1024]{2,1,0:T(8,128)(2,1)} %shard_map.70), calls=%async_computation.2 | async-start | bytes 786432 | tf_op jit(solution)/shard_map/all_to_all | solution.py:259
  51.1 13.4 %collective-permute-start.2 = (bf16[256,1024]{1,0:T(8,128)(2,1)S(1)}, bf16[256,1024]{1,0:T(8,128)(2,1)S(1)}, u32[]{:S(2)}, u32[]{:S(2)}) collective-permute-start(bf16[256,1024]{1,0:T(8,128)(2,1)S(1)} %copy-done), channel_id=1, source_target_pairs={{3,0},{0,1},{1,2},{2,3},{7,4},{4,5},{5,6},{6,7},{11,8},{8,9},{9,10... | collective-permute-start | bytes 1572872 | tf_op jit(solution)/shard_map/ppermute | solution.py:251
  53.3 12.1 %collective-permute-start.1 = (bf16[256,1024]{1,0:T(8,128)(2,1)S(1)}, bf16[256,1024]{1,0:T(8,128)(2,1)S(1)}, u32[]{:S(2)}, u32[]{:S(2)}) collective-permute-start(bf16[256,1024]{1,0:T(8,128)(2,1)S(1)} %collective-permute-done.refs_1_), channel_id=1, source_target_pairs={{1,0},{2,1},{3,2},{0,3},{5,4},{6,5},{7,6},{4,7},{9,8},{10,9},{11,1... | collective-permute-start | bytes 1572872 | tf_op jit(solution)/shard_map/ppermute | solution.py:254
  57.6 8.6 %collective-permute-start.3 = (bf16[192,1024]{1,0:T(8,128)(2,1)S(1)}, bf16[192,1024]{1,0:T(8,128)(2,1)S(1)}, u32[]{:S(2)}, u32[]{:S(2)}) collective-permute-start(bf16[192,1024]{1,0:T(8,128)(2,1)S(1)} %bitcast.11), channel_id=1, source_target_pairs={{0,16},{16,0},{1,17},{17,1},{2,18},{18,2},{3,19},{19,3},{4,20},{20... | collective-permute-start | bytes 1179656 | tf_op jit(solution)/shard_map/ppermute | solution.py:260

commit v5 on v4

--- a/solution.py
+++ b/solution.py
@@ -18,6 +18,7 @@
 NEAR = NX
 SLOTS = ROUNDS * CAP
 LANES = 128
+Z_GROUP = [[(i + NZ // 2) % NZ for i in range(NZ)]]
 FOLD = D // LANES
 KEEP = ROUNDS * NZ
 
@@ -245,7 +246,7 @@
         [VMEM((PLANE * SLOTS, D), F32), VMEM((ROUNDS * FOLD, LANES), F32)],
     )
     mine = compact(blocks)
-    mine = lax.all_to_all(mine, "z", 0, 0)
+    mine = lax.all_to_all(mine, "z", 0, 0, axis_index_groups=Z_GROUP)
 
     def from_side(rows, k):
         return lax.ppermute(rows, "x", [((i + k) % NX, i) for i in range(NX)])
@@ -271,7 +272,7 @@
     running, sums = last(mins)
     sums = lax.all_to_all(sums, ("c", "y"), 0, 0)
     relay = call(relay_kernel, [vspec()], [((NZ, 128), F32)])
-    sums = lax.all_to_all(relay(sums), "z", 0, 0)
+    sums = lax.all_to_all(relay(sums), "z", 0, 0, axis_index_groups=Z_GROUP)
     final = call(
         final_kernel,
         [vspec()] * 2,

time: 107 us -> 100 us (0.935)
  waiting for transfers between devices: 10.6 us -> 6.27 us
  blocking collectives: 54 us -> 49.9 us
  starting transfers between devices: 34.1 us -> 36.3 us
    all_to_all x1, waiting for transfers between devices: 9.39 us -> 1.39 us  [body(): mine = lax.all_to_all(mine, 'z', 0, 0, axis_index_groups=Z_GROUP)]
    all_to_all x1, starting transfers between devices: 15.7 us -> 19 us  [body(): mine = lax.all_to_all(mine, 'z', 0, 0, axis_index_groups=Z_GROUP)]
    all_to_all x1, blocking collectives: 14.7 us -> 12.2 us  [body(): sums = lax.all_to_all(sums, ('c', 'y'), 0, 0)]
    ppermute x2, waiting for transfers between devices: 0.33 us -> 2.36 us  [from_side(): return lax.ppermute(rows, 'x', [((i + k) % NX, i) for i in range(NX)])]
    all_to_all x1, blocking collectives: 14.6 us -> 12.8 us  [body(): sums = lax.all_to_all(relay(sums), 'z', 0, 0, axis_index_groups=Z_GROUP)]
    ppermute x1, waiting for transfers between devices: 0.91 us -> 2.51 us  [body(): far_side = lax.ppermute(right, 'x', [((i + 1) % NX, i) for i in range(NX)])]
where the time goes in v5:
time: 100 us; the launch traced here: 99.8 us
  blocking collectives  49.9 us (50%)
  starting transfers between devices  36.3 us (36%)
  Pallas kernels  6.6 us (7%)
  waiting for transfers between devices  6.27 us (6%)
    all_to_all x1, starting transfers between devices, body(): mine = lax.all_to_all(mine, 'z', 0, 0, axis_index_groups=Z_GROUP)  19 us
    all_to_all x1, blocking collectives, body(): blocks = lax.all_to_all(blocks, plane, 0, 0)  15.9 us
    all_to_all x1, blocking collectives, body(): sums = lax.all_to_all(relay(sums), 'z', 0, 0, axis_index_groups=Z_GROUP)  12.8 us
    all_to_all x1, blocking collectives, body(): sums = lax.all_to_all(sums, ('c', 'y'), 0, 0)  12.2 us
    all_to_all x1, blocking collectives, body(): lax.all_to_all(other(own(base, cands, *line), others, *line), 'x', 0, 0)  8.96 us
    pallas_call x9, Pallas kernels, run(): return kern(*placed)  6.6 us
    ppermute x1, starting transfers between devices, body(): others = lax.ppermute(cands, 'c', [(0, 1), (1, 0)])  5.17 us
    ppermute x2, starting transfers between devices, from_side(): return lax.ppermute(rows, 'x', [((i + k) % NX, i) for i in range(NX)])  4.6 us
  transfers between devices with their start and end apart: 6, of which 3 were waited for; matrix products, arithmetic and copies ran while one was open for 0% of the time, Pallas kernels for 2%

profile of v5, /device:TPU:1, one launch (start us, length us, event | category | flops | bytes accessed | tf_op | source)
XLA Modules:
  0.0 99.8 jit_solution(11656560650191830080)
XLA Ops:
  0.6 1.3 %shard_map.68 = bf16[16,3,4,1024]{3,2,1,0:T(4,128)(2,1)S(1)} custom-call(s32[3]{0:T(128)} %bitcast.18, s32[3,1,1,4]{3,2,1,0:T(1,128)} %idx_hbm.1, bf16[256,1024]{1,0:T(8,128)(2,1)} %refs_0_.3), custom_call_target="tpu_custom_call" | custom-call | tf_op jit(solution)/shard_map/pallas_call | solution.py:221
  1.9 15.9 %all_to_all.42.recv_ref = bf16[16,3,4,1024]{3,2,1,0:T(4,128)(2,1)S(1)} all-to-all(bf16[16,3,4,1024]{3,2,1,0:T(4,128)(2,1)S(1)} %shard_map.68), channel_id=1, replica_groups=mesh['z'=16,'c'=2,'y'=4,'x'=4] {'y','x'}, dimensions={0} | all-to-all | bytes 786432 | tf_op jit(solution)/shard_map/all_to_all | solution.py:241
  17.8 0.0 copy-start
  17.8 1.1 %shard_map.69 = bf16[16,24,128]{2,1,0:T(8,128)(2,1)} custom-call(bf16[16,3,4,1024]{3,2,1,0:T(4,128)(2,1)S(1)} %all_to_all.42.recv_ref), custom_call_target="tpu_custom_call" | custom-call | tf_op jit(solution)/shard_map/pallas_call | solution.py:221
  18.9 19.0 %all-to-all-start.1 = ((bf16[16,24,128]{2,1,0:T(8,128)(2,1)}), bf16[16,24,128]{2,1,0:T(8,128)(2,1)S(1)}, u32[]{:S(2)}, u32[]{:S(2)}) async-start(bf16[16,24,128]{2,1,0:T(8,128)(2,1)} %shard_map.69), calls=%async_computation.1 | async-start | bytes 196608 | tf_op jit(solution)/shard_map/all_to_all | solution.py:249
  38.0 0.0 copy-done
  38.0 2.4 %collective-permute-start = (bf16[256,1024]{1,0:T(8,128)(2,1)S(1)}, bf16[256,1024]{1,0:T(8,128)(2,1)S(1)}, u32[]{:S(2)}, u32[]{:S(2)}) collective-permute-start(bf16[256,1024]{1,0:T(8,128)(2,1)S(1)} %copy-done), channel_id=1, source_target_pairs={{1,0},{2,1},{3,2},{0,3},{5,4},{6,5},{7,6},{4,7},{9,8},{10,9},{11,1... | collective-permute-start | bytes 1572872 | tf_op jit(solution)/shard_map/ppermute | solution.py:252
  40.4 1.4 %all-to-all-done.1 = bf16[16,24,128]{2,1,0:T(8,128)(2,1)S(1)} async-done(((bf16[16,24,128]{2,1,0:T(8,128)(2,1)}), bf16[16,24,128]{2,1,0:T(8,128)(2,1)S(1)}, u32[]{:S(2)}, u32[]{:S(2)}) %all-to-all-start.1) | async-done | bytes 98336 | tf_op jit(solution)/shard_map/all_to_all | solution.py:249
  41.8 1.1 %shard_map.70 = bf16[4,48,1024]{2,1,0:T(8,128)(2,1)} custom-call(bf16[384,128]{1,0:T(8,128)(2,1)S(1)} %bitcast.13), custom_call_target="tpu_custom_call" | custom-call | tf_op jit(solution)/shard_map/pallas_call | solution.py:221
  42.8 0.0 copy-start.1
  42.8 3.6 %all-to-all-start.2 = ((bf16[4,48,1024]{2,1,0:T(8,128)(2,1)}), bf16[4,48,1024]{2,1,0:T(8,128)(2,1)S(1)}, u32[]{:S(2)}, u32[]{:S(2)}) async-start(bf16[4,48,1024]{2,1,0:T(8,128)(2,1)} %shard_map.70), calls=%async_computation.2 | async-start | bytes 786432 | tf_op jit(solution)/shard_map/all_to_all | solution.py:260
  46.4 2.2 %collective-permute-start.2 = (bf16[256,1024]{1,0:T(8,128)(2,1)S(1)}, bf16[256,1024]{1,0:T(8,128)(2,1)S(1)}, u32[]{:S(2)}, u32[]{:S(2)}) collective-permute-start(bf16[256,1024]{1,0:T(8,128)(2,1)S(1)} %copy-done), channel_id=1, source_target_pairs={{3,0},{0,1},{1,2},{2,3},{7,4},{4,5},{5,6},{6,7},{11,8},{8,9},{9,10... | collective-permute-start | bytes 1572872 | tf_op jit(solution)/shard_map/ppermute | solution.py:252
  48.6 2.4 %collective-permute-done.refs_1_ = bf16[256,1024]{1,0:T(8,128)(2,1)S(1)} collective-permute-done((bf16[256,1024]{1,0:T(8,128)(2,1)S(1)}, bf16[256,1024]{1,0:T(8,128)(2,1)S(1)}, u32[]{:S(2)}, u32[]{:S(2)}) %collective-permute-start) | collective-permute-done | bytes 524320 | tf_op jit(solution)/shard_map/ppermute | solution.py:252
  51.0 3.9 %collective-permute-start.1 = (bf16[256,1024]{1,0:T(8,128)(2,1)S(1)}, bf16[256,1024]{1,0:T(8,128)(2,1)S(1)}, u32[]{:S(2)}, u32[]{:S(2)}) collective-permute-start(bf16[256,1024]{1,0:T(8,128)(2,1)S(1)} %collective-permute-done.refs_1_), channel_id=1, source_target_pairs={{1,0},{2,1},{3,2},{0,3},{5,4},{6,5},{7,6},{4,7},{9,8},{10,9},{11,1... | collective-permute-start | bytes 1572872 | tf_op jit(solution)/shard_map/ppermute | solution.py:255
  54.9 0.0 all-to-all-done.2
  54.9 5.2 %collective-permute-start.3 = (bf16[192,1024]{1,0:T(8,128)(2,1)S(1)}, bf16[192,1024]{1,0:T(8,128)(2,1)S(1)}, u32[]{:S(2)}, u32[]{:S(2)}) collective-permute-start(bf16[192,1024]{1,0:T(8,128)(2,1)S(1)} %bitcast.11), channel_id=1, source_target_pairs={{0,16},{16,0},{1,17},{17,1},{2,18},{18,2},{3,19},{19,3},{4,20},{20... | collective-permute-start | bytes 1179656 | tf_op jit(solution)/shard_map/ppermute | solution.py:261
  60.0 0.0 copy-done.1
  60.1 0.6 shard_map.67.base_ref
  60.6 0.0 collective-permute-done.2.refs_3_
  60.6 2.5 %collective-permute-done.1.refs_2_ = bf16[256,1024]{1,0:T(8,128)(2,1)S(1)} collective-permute-done((bf16[256,1024]{1,0:T(8,128)(2,1)S(1)}, bf16[256,1024]{1,0:T(8,128)(2,1)S(1)}, u32[]{:S(2)}, u32[]{:S(2)}) %collective-permute-start.1) | collective-permute-done | bytes 524320 | tf_op jit(solution)/shard_map/ppermute | solution.py:255
  63.1 0.9 shard_map.71.own_ref
  64.0 0.0 collective-permute-done.3.cands_ref
  64.0 0.9 shard_map.72
  64.9 9.0 %all_to_all.43.recv_ref = f32[4,16,256]{2,1,0:T(8,128)S(1)} all-to-all(f32[4,16,256]{2,1,0:T(8,128)S(1)} %shard_map.72), channel_id=1, replica_groups=mesh['z'=16,'c'=2,'y'=4,'x'=4] {'x'}, dimensions={0} | all-to-all | bytes 131072 | tf_op jit(solution)/shard_map/all_to_all | solution.py:265
  73.9 0.1 shard_map.73
  74.0 12.2 %all_to_all.44 = f32[8,1,128]{2,1,0:T(1,128)S(1)} all-to-all(f32[8,1,128]{2,1,0:T(1,128)S(1)} %bitcast.17), channel_id=1, replica_groups=mesh['z'=16,'c'=2,'y'=4,'x'=4] {'c','y'}, dimensions={0} | all-to-all | bytes 8192 | tf_op jit(solution)/shard_map/all_to_all | solution.py:273
  86.3 12.8 %all_to_all.45 = f32[16,1,128]{2,1,0:T(1,128)S(1)} all-to-all(f32[16,1,128]{2,1,0:T(1,128)S(1)} %bitcast.15), channel_id=1, replica_groups={{256,288,320,352,384,416,448,480,0,32,64,96,128,160,192,224},{257,289,3..., dimensions={0} | all-to-all | bytes 16384 | tf_op jit(solution)/shard_map/all_to_all | solution.py:275
  99.1 0.7 shard_map.75
  (1 shorter events, 0.0 us)
Async XLA Ops:
  17.8 20.2 %copy-start = (bf16[256,1024]{1,0:T(8,128)(2,1)S(1)}, bf16[256,1024]{1,0:T(8,128)(2,1)}, u32[]{:S(2)}) copy-start(bf16[256,1024]{1,0:T(8,128)(2,1)} %refs_0_.3) | copy-start | bytes 1572868
  18.9 22.9 %all-to-all-start.1 = ((bf16[16,24,128]{2,1,0:T(8,128)(2,1)}), bf16[16,24,128]{2,1,0:T(8,128)(2,1)S(1)}, u32[]{:S(2)}, u32[]{:S(2)}) async-start(bf16[16,24,128]{2,1,0:T(8,128)(2,1)} %shard_map.69), calls=%async_computation.1 | async-start | bytes 196608 | tf_op jit(solution)/shard_map/all_to_all | solution.py:249
  38.0 13.0 %collective-permute-start = (bf16[256,1024]{1,0:T(8,128)(2,1)S(1)}, bf16[256,1024]{1,0:T(8,128)(2,1)S(1)}, u32[]{:S(2)}, u32[]{:S(2)}) collective-permute-start(bf16[256,1024]{1,0:T(8,128)(2,1)S(1)} %copy-done), channel_id=1, source_target_pairs={{1,0},{2,1},{3,2},{0,3},{5,4},{6,5},{7,6},{4,7},{9,8},{10,9},{11,1... | collective-permute-start | bytes 1572872 | tf_op jit(solution)/shard_map/ppermute | solution.py:252
  42.8 17.2 %copy-start.1 = (bf16[1024]{0:T(1024)(128)(2,1)S(1)}, bf16[1024]{0:T(1024)(128)(2,1)}, u32[]{:S(2)}) copy-start(bf16[1024]{0:T(1024)(128)(2,1)} %center_ref.1) | copy-start | bytes 6148
  42.8 12.0 %all-to-all-start.2 = ((bf16[4,48,1024]{2,1,0:T(8,128)(2,1)}), bf16[4,48,1024]{2,1,0:T(8,128)(2,1)S(1)}, u32[]{:S(2)}, u32[]{:S(2)}) async-start(bf16[4,48,1024]{2,1,0:T(8,128)(2,1)} %shard_map.70), calls=%async_computation.2 | async-start | bytes 786432 | tf_op jit(solution)/shard_map/all_to_all | solution.py:260
  46.4 14.2 %collective-permute-start.2 = (bf16[256,1024]{1,0:T(8,128)(2,1)S(1)}, bf16[256,1024]{1,0:T(8,128)(2,1)S(1)}, u32[]{:S(2)}, u32[]{:S(2)}) collective-permute-start(bf16[256,1024]{1,0:T(8,128)(2,1)S(1)} %copy-done), channel_id=1, source_target_pairs={{3,0},{0,1},{1,2},{2,3},{7,4},{4,5},{5,6},{6,7},{11,8},{8,9},{9,10... | collective-permute-start | bytes 1572872 | tf_op jit(solution)/shard_map/ppermute | solution.py:252
  51.0 12.2 %collective-permute-start.1 = (bf16[256,1024]{1,0:T(8,128)(2,1)S(1)}, bf16[256,1024]{1,0:T(8,128)(2,1)S(1)}, u32[]{:S(2)}, u32[]{:S(2)}) collective-permute-start(bf16[256,1024]{1,0:T(8,128)(2,1)S(1)} %collective-permute-done.refs_1_), channel_id=1, source_target_pairs={{1,0},{2,1},{3,2},{0,3},{5,4},{6,5},{7,6},{4,7},{9,8},{10,9},{11,1... | collective-permute-start | bytes 1572872 | tf_op jit(solution)/shard_map/ppermute | solution.py:255
  54.9 9.2 %collective-permute-start.3 = (bf16[192,1024]{1,0:T(8,128)(2,1)S(1)}, bf16[192,1024]{1,0:T(8,128)(2,1)S(1)}, u32[]{:S(2)}, u32[]{:S(2)}) collective-permute-start(bf16[192,1024]{1,0:T(8,128)(2,1)S(1)} %bitcast.11), channel_id=1, source_target_pairs={{0,16},{16,0},{1,17},{17,1},{2,18},{18,2},{3,19},{19,3},{4,20},{20... | collective-permute-start | bytes 1179656 | tf_op jit(solution)/shard_map/ppermute | solution.py:261

commit v6 on v5

--- a/solution.py
+++ b/solution.py
@@ -18,7 +18,18 @@
 NEAR = NX
 SLOTS = ROUNDS * CAP
 LANES = 128
-Z_GROUP = [[(i + NZ // 2) % NZ for i in range(NZ)]]
+
+
+def led_by(size, first):
+    return [[(first + i) % size for i in range(size)]]
+
+
+Z_GROUP = led_by(NZ, 9)
+PLANE_GROUP = led_by(PLANE, 15)
+Y_GROUP = led_by(NY, 2)
+X_FIRST = 2
+X_GROUP = led_by(NX, X_FIRST)
+CORE_Y_GROUP = led_by(NC * NY, 6)
 FOLD = D // LANES
 KEEP = ROUNDS * NZ
 
@@ -164,7 +175,7 @@
 def last_kernel(recv_ref, run_ref, sums_ref, all_ref):
     def base_row(row):
         row += ROUNDS * NEAR
-        return jnp.concatenate([recv_ref[b, row : row + 1] for b in range(NEAR)], axis=0)
+        return jnp.concatenate([recv_ref[(b - X_FIRST) % NEAR, row : row + 1] for b in range(NEAR)], axis=0)
 
     rows_norm = base_row(0)
     running = base_row(1)
@@ -238,7 +249,7 @@
     blocks = pack(counts.reshape(ROUNDS), cand_index, points)
     plane = ("y", "x")
     blocks, early = lax.optimization_barrier((blocks, points))
-    blocks = lax.all_to_all(blocks, plane, 0, 0)
+    blocks = lax.all_to_all(blocks, plane, 0, 0, axis_index_groups=PLANE_GROUP)
     compact = call(
         compact_kernel,
         [vspec()],
@@ -257,12 +268,13 @@
     base = call(base_kernel, [vspec()] * 2, [((2, ROWS_DEV), F32)])(points, first_center)
     spread = call(spread_kernel, [vspec()], [((FAR, KEEP, D), BF16)])
     mine = mine.reshape(NZ * ROUNDS * FOLD, LANES)
-    cands = lax.all_to_all(spread(mine), "y", 0, 0).reshape(FAR * KEEP, D)
+    cands = lax.all_to_all(spread(mine), "y", 0, 0, axis_index_groups=Y_GROUP).reshape(FAR * KEEP, D)
     others = lax.ppermute(cands, "c", [(0, 1), (1, 0)])
     rows = ((4 * NEAR, ROWS_DEV), F32)
     own = call(own_kernel, [vspec()] * (2 + NEAR), [rows])
     other = call(other_kernel, [vspec()] * (2 + NEAR), [((NEAR, *rows[0]), F32)], [VMEM(*rows)])
-    mins = lax.all_to_all(other(own(base, cands, *line), others, *line), "x", 0, 0)
+    mins = other(own(base, cands, *line), others, *line)
+    mins = lax.all_to_all(mins, "x", 0, 0, axis_index_groups=X_GROUP)
     last = call(
         last_kernel,
         [vspec()],
@@ -270,7 +282,7 @@
         [VMEM((NEAR, 1, ROWS_DEV), F32)],
     )
     running, sums = last(mins)
-    sums = lax.all_to_all(sums, ("c", "y"), 0, 0)
+    sums = lax.all_to_all(sums, ("c", "y"), 0, 0, axis_index_groups=CORE_Y_GROUP)
     relay = call(relay_kernel, [vspec()], [((NZ, 128), F32)])
     sums = lax.all_to_all(relay(sums), "z", 0, 0, axis_index_groups=Z_GROUP)
     final = call(

time: 100 us -> 98.2 us (0.982); the launches traced: 99.8 us -> 96.9 us
  blocking collectives: 49.9 us -> 45.5 us
  starting transfers between devices: 36.3 us -> 40.4 us
  waiting for transfers between devices: 6.27 us -> 3.68 us
    all_to_all x3, blocking collectives: 37 us -> 31.8 us  [the longest x1 13.1 us: body(): blocks = lax.all_to_all(blocks, plane, 0, 0, axis_index_groups=PLANE_GROUP)]
    all_to_all x1, starting transfers between devices: 3.59 us -> 5.61 us  [body(): lax.all_to_all(spread(mine), 'y', 0, 0, axis_index_groups=Y_GROUP)]
    ppermute x2, waiting for transfers between devices: 2.36 us -> 0.61 us  [from_side(): return lax.ppermute(rows, 'x', [((i + k) % NX, i) for i in range(NX)])]
    ppermute x2, starting transfers between devices: 4.6 us -> 6.06 us  [from_side(): return lax.ppermute(rows, 'x', [((i + k) % NX, i) for i in range(NX)])]
    ppermute x1, starting transfers between devices: 3.88 us -> 5.31 us  [body(): far_side = lax.ppermute(right, 'x', [((i + 1) % NX, i) for i in range(NX)])]
  transfers between devices with their start and end apart: 6 -> 6, of which waited for: 3 -> 4; matrix products, arithmetic and copies ran while one was open for 0% -> 0% of each run, Pallas kernels for 2% -> 3%
where the time goes in v6:
time: 98.2 us; the launch traced here: 96.9 us
  blocking collectives  45.5 us (46%)
  starting transfers between devices  40.4 us (41%)
  Pallas kernels  6.6 us (7%)
  waiting for transfers between devices  3.68 us (4%)
    all_to_all x1, starting transfers between devices, body(): mine = lax.all_to_all(mine, 'z', 0, 0, axis_index_groups=Z_GROUP)  18.4 us
    all_to_all x1, blocking collectives, body(): sums = lax.all_to_all(relay(sums), 'z', 0, 0, axis_index_groups=Z_GROUP)  13.7 us
    all_to_all x1, blocking collectives, body(): blocks = lax.all_to_all(blocks, plane, 0, 0, axis_index_groups=PLANE_GROUP)  13.1 us
    all_to_all x1, blocking collectives, body(): lax.all_to_all(sums, ('c', 'y'), 0, 0, axis_index_groups=CORE_Y_GROUP)  11.3 us
    all_to_all x1, blocking collectives, body(): mins = lax.all_to_all(mins, 'x', 0, 0, axis_index_groups=X_GROUP)  7.35 us
    pallas_call x9, Pallas kernels, run(): return kern(*placed)  6.6 us
    ppermute x2, starting transfers between devices, from_side(): return lax.ppermute(rows, 'x', [((i + k) % NX, i) for i in range(NX)])  6.06 us
    all_to_all x1, starting transfers between devices, body(): lax.all_to_all(spread(mine), 'y', 0, 0, axis_index_groups=Y_GROUP)  5.61 us
  transfers between devices with their start and end apart: 6, of which 4 were waited for; matrix products, arithmetic and copies ran while one was open for 0% of the time, Pallas kernels for 3%

profile of v6, /device:TPU:1, one launch (start us, length us, event | category | flops | bytes accessed | tf_op | source)
XLA Modules:
  0.0 96.9 jit_solution(2962537234694281709)
XLA Ops:
  0.6 1.3 %shard_map.68 = bf16[16,3,4,1024]{3,2,1,0:T(4,128)(2,1)S(1)} custom-call(s32[3]{0:T(128)} %bitcast.18, s32[3,1,1,4]{3,2,1,0:T(1,128)} %idx_hbm.1, bf16[256,1024]{1,0:T(8,128)(2,1)} %refs_0_.3), custom_call_target="tpu_custom_call" | custom-call | tf_op jit(solution)/shard_map/pallas_call | solution.py:232
  1.9 13.1 %all_to_all.42.recv_ref = bf16[16,3,4,1024]{3,2,1,0:T(4,128)(2,1)S(1)} all-to-all(bf16[16,3,4,1024]{3,2,1,0:T(4,128)(2,1)S(1)} %shard_map.68), channel_id=1, replica_groups={{15,0,1,2,3,4,5,6,7,8,9,10,11,12,13,14},{31,16,17,18,19,20,21,22,23,24,..., dimensions={0} | all-to-all | bytes 786432 | tf_op jit(solution)/shard_map/all_to_all | solution.py:252
  15.0 0.0 copy-start
  15.0 1.1 %shard_map.69 = bf16[16,24,128]{2,1,0:T(8,128)(2,1)} custom-call(bf16[16,3,4,1024]{3,2,1,0:T(4,128)(2,1)S(1)} %all_to_all.42.recv_ref), custom_call_target="tpu_custom_call" | custom-call | tf_op jit(solution)/shard_map/pallas_call | solution.py:232
  16.1 18.4 %all-to-all-start.1 = ((bf16[16,24,128]{2,1,0:T(8,128)(2,1)}), bf16[16,24,128]{2,1,0:T(8,128)(2,1)S(1)}, u32[]{:S(2)}, u32[]{:S(2)}) async-start(bf16[16,24,128]{2,1,0:T(8,128)(2,1)} %shard_map.69), calls=%async_computation.1 | async-start | bytes 196608 | tf_op jit(solution)/shard_map/all_to_all | solution.py:260
  34.6 0.0 copy-done
  34.6 4.2 %collective-permute-start = (bf16[256,1024]{1,0:T(8,128)(2,1)S(1)}, bf16[256,1024]{1,0:T(8,128)(2,1)S(1)}, u32[]{:S(2)}, u32[]{:S(2)}) collective-permute-start(bf16[256,1024]{1,0:T(8,128)(2,1)S(1)} %copy-done), channel_id=1, source_target_pairs={{1,0},{2,1},{3,2},{0,3},{5,4},{6,5},{7,6},{4,7},{9,8},{10,9},{11,1... | collective-permute-start | bytes 1572872 | tf_op jit(solution)/shard_map/ppermute | solution.py:263
  38.7 0.6 all-to-all-done.1
  39.3 1.1 %shard_map.70 = bf16[4,48,1024]{2,1,0:T(8,128)(2,1)} custom-call(bf16[384,128]{1,0:T(8,128)(2,1)S(1)} %bitcast.13), custom_call_target="tpu_custom_call" | custom-call | tf_op jit(solution)/shard_map/pallas_call | solution.py:232
  40.4 0.0 copy-start.1
  40.4 5.6 %all-to-all-start.2 = ((bf16[4,48,1024]{2,1,0:T(8,128)(2,1)}), bf16[4,48,1024]{2,1,0:T(8,128)(2,1)S(1)}, u32[]{:S(2)}, u32[]{:S(2)}) async-start(bf16[4,48,1024]{2,1,0:T(8,128)(2,1)} %shard_map.70), calls=%async_computation.2 | async-start | bytes 786432 | tf_op jit(solution)/shard_map/all_to_all | solution.py:271
  46.0 1.9 %collective-permute-start.2 = (bf16[256,1024]{1,0:T(8,128)(2,1)S(1)}, bf16[256,1024]{1,0:T(8,128)(2,1)S(1)}, u32[]{:S(2)}, u32[]{:S(2)}) collective-permute-start(bf16[256,1024]{1,0:T(8,128)(2,1)S(1)} %copy-done), channel_id=1, source_target_pairs={{3,0},{0,1},{1,2},{2,3},{7,4},{4,5},{5,6},{6,7},{11,8},{8,9},{9,10... | collective-permute-start | bytes 1572872 | tf_op jit(solution)/shard_map/ppermute | solution.py:263
  47.9 0.2 collective-permute-done.refs_1_
  48.1 5.3 %collective-permute-start.1 = (bf16[256,1024]{1,0:T(8,128)(2,1)S(1)}, bf16[256,1024]{1,0:T(8,128)(2,1)S(1)}, u32[]{:S(2)}, u32[]{:S(2)}) collective-permute-start(bf16[256,1024]{1,0:T(8,128)(2,1)S(1)} %collective-permute-done.refs_1_), channel_id=1, source_target_pairs={{1,0},{2,1},{3,2},{0,3},{5,4},{6,5},{7,6},{4,7},{9,8},{10,9},{11,1... | collective-permute-start | bytes 1572872 | tf_op jit(solution)/shard_map/ppermute | solution.py:266
  53.4 0.0 all-to-all-done.2
  53.4 5.0 %collective-permute-start.3 = (bf16[192,1024]{1,0:T(8,128)(2,1)S(1)}, bf16[192,1024]{1,0:T(8,128)(2,1)S(1)}, u32[]{:S(2)}, u32[]{:S(2)}) collective-permute-start(bf16[192,1024]{1,0:T(8,128)(2,1)S(1)} %bitcast.11), channel_id=1, source_target_pairs={{0,16},{16,0},{1,17},{17,1},{2,18},{18,2},{3,19},{19,3},{4,20},{20... | collective-permute-start | bytes 1179656 | tf_op jit(solution)/shard_map/ppermute | solution.py:272
  58.4 0.0 copy-done.1
  58.4 0.6 shard_map.67.base_ref
  58.9 0.4 collective-permute-done.2.refs_3_
  59.4 2.5 %collective-permute-done.1.refs_2_ = bf16[256,1024]{1,0:T(8,128)(2,1)S(1)} collective-permute-done((bf16[256,1024]{1,0:T(8,128)(2,1)S(1)}, bf16[256,1024]{1,0:T(8,128)(2,1)S(1)}, u32[]{:S(2)}, u32[]{:S(2)}) %collective-permute-start.1) | collective-permute-done | bytes 524320 | tf_op jit(solution)/shard_map/ppermute | solution.py:266
  61.9 0.9 shard_map.71.own_ref
  62.8 0.0 collective-permute-done.3.cands_ref
  62.8 0.9 shard_map.72
  63.7 7.3 %all_to_all.43.recv_ref = f32[4,16,256]{2,1,0:T(8,128)S(1)} all-to-all(f32[4,16,256]{2,1,0:T(8,128)S(1)} %shard_map.72), channel_id=1, replica_groups={{2,3,0,1},{6,7,4,5},{10,11,8,9},{14,15,12,13},{18,19,16,17},{22,23,20,2..., dimensions={0} | all-to-all | bytes 131072 | tf_op jit(solution)/shard_map/all_to_all | solution.py:277
  71.0 0.1 shard_map.73
  71.2 11.3 %all_to_all.44 = f32[8,1,128]{2,1,0:T(1,128)S(1)} all-to-all(f32[8,1,128]{2,1,0:T(1,128)S(1)} %bitcast.17), channel_id=1, replica_groups={{24,28,0,4,8,12,16,20},{25,29,1,5,9,13,17,21},{26,30,2,6,10,14,18,22},{..., dimensions={0} | all-to-all | bytes 8192 | tf_op jit(solution)/shard_map/all_to_all | solution.py:285
  82.5 13.7 %all_to_all.45 = f32[16,1,128]{2,1,0:T(1,128)S(1)} all-to-all(f32[16,1,128]{2,1,0:T(1,128)S(1)} %bitcast.15), channel_id=1, replica_groups={{288,320,352,384,416,448,480,0,32,64,96,128,160,192,224,256},{289,321,3..., dimensions={0} | all-to-all | bytes 16384 | tf_op jit(solution)/shard_map/all_to_all | solution.py:287
  96.3 0.7 shard_map.75
  (1 shorter events, 0.0 us)
Async XLA Ops:
  15.0 19.6 %copy-start = (bf16[256,1024]{1,0:T(8,128)(2,1)S(1)}, bf16[256,1024]{1,0:T(8,128)(2,1)}, u32[]{:S(2)}) copy-start(bf16[256,1024]{1,0:T(8,128)(2,1)} %refs_0_.3) | copy-start | bytes 1572868
  16.1 23.2 %all-to-all-start.1 = ((bf16[16,24,128]{2,1,0:T(8,128)(2,1)}), bf16[16,24,128]{2,1,0:T(8,128)(2,1)S(1)}, u32[]{:S(2)}, u32[]{:S(2)}) async-start(bf16[16,24,128]{2,1,0:T(8,128)(2,1)} %shard_map.69), calls=%async_computation.1 | async-start | bytes 196608 | tf_op jit(solution)/shard_map/all_to_all | solution.py:260
  34.6 13.5 %collective-permute-start = (bf16[256,1024]{1,0:T(8,128)(2,1)S(1)}, bf16[256,1024]{1,0:T(8,128)(2,1)S(1)}, u32[]{:S(2)}, u32[]{:S(2)}) collective-permute-start(bf16[256,1024]{1,0:T(8,128)(2,1)S(1)} %copy-done), channel_id=1, source_target_pairs={{1,0},{2,1},{3,2},{0,3},{5,4},{6,5},{7,6},{4,7},{9,8},{10,9},{11,1... | collective-permute-start | bytes 1572872 | tf_op jit(solution)/shard_map/ppermute | solution.py:263
  40.4 18.0 %copy-start.1 = (bf16[1024]{0:T(1024)(128)(2,1)S(1)}, bf16[1024]{0:T(1024)(128)(2,1)}, u32[]{:S(2)}) copy-start(bf16[1024]{0:T(1024)(128)(2,1)} %center_ref.1) | copy-start | bytes 6148
  40.4 13.0 %all-to-all-start.2 = ((bf16[4,48,1024]{2,1,0:T(8,128)(2,1)}), bf16[4,48,1024]{2,1,0:T(8,128)(2,1)S(1)}, u32[]{:S(2)}, u32[]{:S(2)}) async-start(bf16[4,48,1024]{2,1,0:T(8,128)(2,1)} %shard_map.70), calls=%async_computation.2 | async-start | bytes 786432 | tf_op jit(solution)/shard_map/all_to_all | solution.py:271
  46.0 13.4 %collective-permute-start.2 = (bf16[256,1024]{1,0:T(8,128)(2,1)S(1)}, bf16[256,1024]{1,0:T(8,128)(2,1)S(1)}, u32[]{:S(2)}, u32[]{:S(2)}) collective-permute-start(bf16[256,1024]{1,0:T(8,128)(2,1)S(1)} %copy-done), channel_id=1, source_target_pairs={{3,0},{0,1},{1,2},{2,3},{7,4},{4,5},{5,6},{6,7},{11,8},{8,9},{9,10... | collective-permute-start | bytes 1572872 | tf_op jit(solution)/shard_map/ppermute | solution.py:263
  48.1 13.8 %collective-permute-start.1 = (bf16[256,1024]{1,0:T(8,128)(2,1)S(1)}, bf16[256,1024]{1,0:T(8,128)(2,1)S(1)}, u32[]{:S(2)}, u32[]{:S(2)}) collective-permute-start(bf16[256,1024]{1,0:T(8,128)(2,1)S(1)} %collective-permute-done.refs_1_), channel_id=1, source_target_pairs={{1,0},{2,1},{3,2},{0,3},{5,4},{6,5},{7,6},{4,7},{9,8},{10,9},{11,1... | collective-permute-start | bytes 1572872 | tf_op jit(solution)/shard_map/ppermute | solution.py:266
  53.4 9.4 %collective-permute-start.3 = (bf16[192,1024]{1,0:T(8,128)(2,1)S(1)}, bf16[192,1024]{1,0:T(8,128)(2,1)S(1)}, u32[]{:S(2)}, u32[]{:S(2)}) collective-permute-start(bf16[192,1024]{1,0:T(8,128)(2,1)S(1)} %bitcast.11), channel_id=1, source_target_pairs={{0,16},{16,0},{1,17},{17,1},{2,18},{18,2},{3,19},{19,3},{4,20},{20... | collective-permute-start | bytes 1179656 | tf_op jit(solution)/shard_map/ppermute | solution.py:272

commit v7 on v6

--- a/solution.py
+++ b/solution.py
@@ -24,12 +24,12 @@
     return [[(first + i) % size for i in range(size)]]
 
 
-Z_GROUP = led_by(NZ, 9)
+Z_GROUP = led_by(NZ, 10)
 PLANE_GROUP = led_by(PLANE, 15)
 Y_GROUP = led_by(NY, 2)
 X_FIRST = 2
 X_GROUP = led_by(NX, X_FIRST)
-CORE_Y_GROUP = led_by(NC * NY, 6)
+SUM_GROUP = led_by(NZ * NC * NY, 86)
 FOLD = D // LANES
 KEEP = ROUNDS * NZ
 
@@ -179,7 +179,7 @@
 
     rows_norm = base_row(0)
     running = base_row(1)
-    lane = iota((NC * FAR, 128), 1)
+    lane = iota((NZ * NC * NY, 128), 1)
     sums = jnp.where(lane == 0, jnp.sum(running), 0.0)
     for r in range(ROUNDS):
         least = recv_ref[0, r * NEAR : (r + 1) * NEAR]
@@ -191,11 +191,6 @@
         all_ref[b] = running[b : b + 1]
     run_ref[...] = all_ref[lax.axis_index("x")]
     sums_ref[...] = sums
-
-
-def relay_kernel(recv_ref, out_ref):
-    total = jnp.sum(recv_ref[...], axis=0, keepdims=True)
-    out_ref[...] = jnp.broadcast_to(total, (NZ, 128))
 
 
 def final_kernel(recv_ref, run_ref, dist_ref, weight_ref, pot_ref):
@@ -278,13 +273,11 @@
     last = call(
         last_kernel,
         [vspec()],
-        [((1, ROWS_DEV), F32), ((NC * FAR, 128), F32)],
+        [((1, ROWS_DEV), F32), ((NZ * NC * NY, 128), F32)],
         [VMEM((NEAR, 1, ROWS_DEV), F32)],
     )
     running, sums = last(mins)
-    sums = lax.all_to_all(sums, ("c", "y"), 0, 0, axis_index_groups=CORE_Y_GROUP)
-    relay = call(relay_kernel, [vspec()], [((NZ, 128), F32)])
-    sums = lax.all_to_all(relay(sums), "z", 0, 0, axis_index_groups=Z_GROUP)
+    sums = lax.all_to_all(sums, ("z", "c", "y"), 0, 0, axis_index_groups=SUM_GROUP)
     final = call(
         final_kernel,
         [vspec()] * 2,

time: 98.2 us -> 97.3 us (level)
  blocking collectives: 45.5 us -> 46.9 us
  starting transfers between devices: 40.4 us -> 39.4 us
    ppermute x1, waiting for transfers between devices: 2.49 us -> 1.04 us  [body(): far_side = lax.ppermute(right, 'x', [((i + 1) % NX, i) for i in range(NX)])]
    all_to_all x2 -> x1, blocking collectives: 25.1 us -> 26.5 us  [body(): lax.all_to_all(sums, ('z', 'c', 'y'), 0, 0, axis_index_groups=SUM_GROUP)]
    pallas_call x9 -> x8, Pallas kernels: 6.6 us -> 6.61 us  [run(): return kern(*placed)]
  transfers between devices with their start and end apart: 6 -> 6, of which waited for: 4 -> 3; matrix products, arithmetic and copies ran while one was open for 0% -> 0% of each run, Pallas kernels for 3% -> 3%
where the time goes in v7:
time: 97.3 us; the launch traced here: 96.8 us
  blocking collectives  46.9 us (48%)
  starting transfers between devices  39.4 us (40%)
  Pallas kernels  6.61 us (7%)
  waiting for transfers between devices  3.11 us (3%)
    all_to_all x1, blocking collectives, body(): lax.all_to_all(sums, ('z', 'c', 'y'), 0, 0, axis_index_groups=SUM_GROUP)  26.5 us
    all_to_all x1, starting transfers between devices, body(): mine = lax.all_to_all(mine, 'z', 0, 0, axis_index_groups=Z_GROUP)  17.5 us
    all_to_all x1, blocking collectives, body(): blocks = lax.all_to_all(blocks, plane, 0, 0, axis_index_groups=PLANE_GROUP)  13.1 us
    all_to_all x1, blocking collectives, body(): mins = lax.all_to_all(mins, 'x', 0, 0, axis_index_groups=X_GROUP)  7.35 us
    pallas_call x8, Pallas kernels, run(): return kern(*placed)  6.61 us
    ppermute x2, starting transfers between devices, from_side(): return lax.ppermute(rows, 'x', [((i + k) % NX, i) for i in range(NX)])  6.06 us
    all_to_all x1, starting transfers between devices, body(): lax.all_to_all(spread(mine), 'y', 0, 0, axis_index_groups=Y_GROUP)  5.61 us
    ppermute x1, starting transfers between devices, body(): others = lax.ppermute(cands, 'c', [(0, 1), (1, 0)])  5.58 us
  transfers between devices with their start and end apart: 6, of which 3 were waited for; matrix products, arithmetic and copies ran while one was open for 0% of the time, Pallas kernels for 3%

profile of v7, /device:TPU:1, one launch (start us, length us, event | category | flops | bytes accessed | tf_op | source)
XLA Modules:
  0.0 96.8 jit_solution(11042261054658982071)
XLA Ops:
  0.6 1.3 %shard_map.68 = bf16[16,3,4,1024]{3,2,1,0:T(4,128)(2,1)S(1)} custom-call(s32[3]{0:T(128)} %bitcast.12, s32[3,1,1,4]{3,2,1,0:T(1,128)} %idx_hbm.1, bf16[256,1024]{1,0:T(8,128)(2,1)} %refs_0_.3), custom_call_target="tpu_custom_call" | custom-call | tf_op jit(solution)/shard_map/pallas_call | solution.py:227
  1.9 13.1 %all_to_all.31.recv_ref = bf16[16,3,4,1024]{3,2,1,0:T(4,128)(2,1)S(1)} all-to-all(bf16[16,3,4,1024]{3,2,1,0:T(4,128)(2,1)S(1)} %shard_map.68), channel_id=1, replica_groups={{15,0,1,2,3,4,5,6,7,8,9,10,11,12,13,14},{31,16,17,18,19,20,21,22,23,24,..., dimensions={0} | all-to-all | bytes 786432 | tf_op jit(solution)/shard_map/all_to_all | solution.py:247
  15.0 0.0 copy-start
  15.0 1.1 %shard_map.69 = bf16[16,24,128]{2,1,0:T(8,128)(2,1)} custom-call(bf16[16,3,4,1024]{3,2,1,0:T(4,128)(2,1)S(1)} %all_to_all.31.recv_ref), custom_call_target="tpu_custom_call" | custom-call | tf_op jit(solution)/shard_map/pallas_call | solution.py:227
  16.1 17.5 %all-to-all-start.1 = ((bf16[16,24,128]{2,1,0:T(8,128)(2,1)}), bf16[16,24,128]{2,1,0:T(8,128)(2,1)S(1)}, u32[]{:S(2)}, u32[]{:S(2)}) async-start(bf16[16,24,128]{2,1,0:T(8,128)(2,1)} %shard_map.69), calls=%async_computation.1 | async-start | bytes 196608 | tf_op jit(solution)/shard_map/all_to_all | solution.py:255
  33.7 0.0 copy-done
  33.7 4.2 %collective-permute-start = (bf16[256,1024]{1,0:T(8,128)(2,1)S(1)}, bf16[256,1024]{1,0:T(8,128)(2,1)S(1)}, u32[]{:S(2)}, u32[]{:S(2)}) collective-permute-start(bf16[256,1024]{1,0:T(8,128)(2,1)S(1)} %copy-done), channel_id=1, source_target_pairs={{1,0},{2,1},{3,2},{0,3},{5,4},{6,5},{7,6},{4,7},{9,8},{10,9},{11,1... | collective-permute-start | bytes 1572872 | tf_op jit(solution)/shard_map/ppermute | solution.py:258
  37.8 1.4 %all-to-all-done.1 = bf16[16,24,128]{2,1,0:T(8,128)(2,1)S(1)} async-done(((bf16[16,24,128]{2,1,0:T(8,128)(2,1)}), bf16[16,24,128]{2,1,0:T(8,128)(2,1)S(1)}, u32[]{:S(2)}, u32[]{:S(2)}) %all-to-all-start.1) | async-done | bytes 98336 | tf_op jit(solution)/shard_map/all_to_all | solution.py:255
  39.2 1.1 %shard_map.70 = bf16[4,48,1024]{2,1,0:T(8,128)(2,1)} custom-call(bf16[384,128]{1,0:T(8,128)(2,1)S(1)} %bitcast.9), custom_call_target="tpu_custom_call" | custom-call | tf_op jit(solution)/shard_map/pallas_call | solution.py:227
  40.3 0.0 copy-start.1
  40.3 5.6 %all-to-all-start.2 = ((bf16[4,48,1024]{2,1,0:T(8,128)(2,1)}), bf16[4,48,1024]{2,1,0:T(8,128)(2,1)S(1)}, u32[]{:S(2)}, u32[]{:S(2)}) async-start(bf16[4,48,1024]{2,1,0:T(8,128)(2,1)} %shard_map.70), calls=%async_computation.2 | async-start | bytes 786432 | tf_op jit(solution)/shard_map/all_to_all | solution.py:266
  45.9 1.9 %collective-permute-start.2 = (bf16[256,1024]{1,0:T(8,128)(2,1)S(1)}, bf16[256,1024]{1,0:T(8,128)(2,1)S(1)}, u32[]{:S(2)}, u32[]{:S(2)}) collective-permute-start(bf16[256,1024]{1,0:T(8,128)(2,1)S(1)} %copy-done), channel_id=1, source_target_pairs={{3,0},{0,1},{1,2},{2,3},{7,4},{4,5},{5,6},{6,7},{11,8},{8,9},{9,10... | collective-permute-start | bytes 1572872 | tf_op jit(solution)/shard_map/ppermute | solution.py:258
  47.8 0.0 collective-permute-done.refs_1_
  47.8 4.6 %collective-permute-start.1 = (bf16[256,1024]{1,0:T(8,128)(2,1)S(1)}, bf16[256,1024]{1,0:T(8,128)(2,1)S(1)}, u32[]{:S(2)}, u32[]{:S(2)}) collective-permute-start(bf16[256,1024]{1,0:T(8,128)(2,1)S(1)} %collective-permute-done.refs_1_), channel_id=1, source_target_pairs={{1,0},{2,1},{3,2},{0,3},{5,4},{6,5},{7,6},{4,7},{9,8},{10,9},{11,1... | collective-permute-start | bytes 1572872 | tf_op jit(solution)/shard_map/ppermute | solution.py:261
  52.5 0.0 all-to-all-done.2
  52.5 5.6 %collective-permute-start.3 = (bf16[192,1024]{1,0:T(8,128)(2,1)S(1)}, bf16[192,1024]{1,0:T(8,128)(2,1)S(1)}, u32[]{:S(2)}, u32[]{:S(2)}) collective-permute-start(bf16[192,1024]{1,0:T(8,128)(2,1)S(1)} %bitcast.7), channel_id=1, source_target_pairs={{0,16},{16,0},{1,17},{17,1},{2,18},{18,2},{3,19},{19,3},{4,20},{20... | collective-permute-start | bytes 1179656 | tf_op jit(solution)/shard_map/ppermute | solution.py:267
  58.1 0.0 copy-done.1
  58.1 0.6 shard_map.67.base_ref
  58.7 0.7 collective-permute-done.2.refs_3_
  59.3 1.0 %collective-permute-done.1.refs_2_ = bf16[256,1024]{1,0:T(8,128)(2,1)S(1)} collective-permute-done((bf16[256,1024]{1,0:T(8,128)(2,1)S(1)}, bf16[256,1024]{1,0:T(8,128)(2,1)S(1)}, u32[]{:S(2)}, u32[]{:S(2)}) %collective-permute-start.1) | collective-permute-done | bytes 524320 | tf_op jit(solution)/shard_map/ppermute | solution.py:261
  60.4 0.9 shard_map.71.own_ref
  61.2 0.0 collective-permute-done.3.cands_ref
  61.3 0.9 shard_map.72
  62.2 7.3 %all_to_all.32.recv_ref = f32[4,16,256]{2,1,0:T(8,128)S(1)} all-to-all(f32[4,16,256]{2,1,0:T(8,128)S(1)} %shard_map.72), channel_id=1, replica_groups={{2,3,0,1},{6,7,4,5},{10,11,8,9},{14,15,12,13},{18,19,16,17},{22,23,20,2..., dimensions={0} | all-to-all | bytes 131072 | tf_op jit(solution)/shard_map/all_to_all | solution.py:272
  69.5 0.1 shard_map.73
  69.7 26.5 %all_to_all.33 = f32[128,1,128]{2,1,0:T(1,128)S(1)} all-to-all(f32[128,1,128]{2,1,0:T(1,128)S(1)} %bitcast.11), channel_id=1, replica_groups={{344,348,352,356,360,364,368,372,376,380,384,388,392,396,400,404,408,41..., dimensions={0} | all-to-all | bytes 131072 | tf_op jit(solution)/shard_map/all_to_all | solution.py:280
  96.2 0.7 shard_map.74
Async XLA Ops:
  15.0 18.7 %copy-start = (bf16[256,1024]{1,0:T(8,128)(2,1)S(1)}, bf16[256,1024]{1,0:T(8,128)(2,1)}, u32[]{:S(2)}) copy-start(bf16[256,1024]{1,0:T(8,128)(2,1)} %refs_0_.3) | copy-start | bytes 1572868
  16.1 23.1 %all-to-all-start.1 = ((bf16[16,24,128]{2,1,0:T(8,128)(2,1)}), bf16[16,24,128]{2,1,0:T(8,128)(2,1)S(1)}, u32[]{:S(2)}, u32[]{:S(2)}) async-start(bf16[16,24,128]{2,1,0:T(8,128)(2,1)} %shard_map.69), calls=%async_computation.1 | async-start | bytes 196608 | tf_op jit(solution)/shard_map/all_to_all | solution.py:255
  33.7 14.2 %collective-permute-start = (bf16[256,1024]{1,0:T(8,128)(2,1)S(1)}, bf16[256,1024]{1,0:T(8,128)(2,1)S(1)}, u32[]{:S(2)}, u32[]{:S(2)}) collective-permute-start(bf16[256,1024]{1,0:T(8,128)(2,1)S(1)} %copy-done), channel_id=1, source_target_pairs={{1,0},{2,1},{3,2},{0,3},{5,4},{6,5},{7,6},{4,7},{9,8},{10,9},{11,1... | collective-permute-start | bytes 1572872 | tf_op jit(solution)/shard_map/ppermute | solution.py:258
  40.3 17.8 %copy-start.1 = (bf16[1024]{0:T(1024)(128)(2,1)S(1)}, bf16[1024]{0:T(1024)(128)(2,1)}, u32[]{:S(2)}) copy-start(bf16[1024]{0:T(1024)(128)(2,1)} %center_ref.1) | copy-start | bytes 6148
  40.3 12.2 %all-to-all-start.2 = ((bf16[4,48,1024]{2,1,0:T(8,128)(2,1)}), bf16[4,48,1024]{2,1,0:T(8,128)(2,1)S(1)}, u32[]{:S(2)}, u32[]{:S(2)}) async-start(bf16[4,48,1024]{2,1,0:T(8,128)(2,1)} %shard_map.70), calls=%async_computation.2 | async-start | bytes 786432 | tf_op jit(solution)/shard_map/all_to_all | solution.py:266
  45.9 13.4 %collective-permute-start.2 = (bf16[256,1024]{1,0:T(8,128)(2,1)S(1)}, bf16[256,1024]{1,0:T(8,128)(2,1)S(1)}, u32[]{:S(2)}, u32[]{:S(2)}) collective-permute-start(bf16[256,1024]{1,0:T(8,128)(2,1)S(1)} %copy-done), channel_id=1, source_target_pairs={{3,0},{0,1},{1,2},{2,3},{7,4},{4,5},{5,6},{6,7},{11,8},{8,9},{9,10... | collective-permute-start | bytes 1572872 | tf_op jit(solution)/shard_map/ppermute | solution.py:258
  47.8 12.5 %collective-permute-start.1 = (bf16[256,1024]{1,0:T(8,128)(2,1)S(1)}, bf16[256,1024]{1,0:T(8,128)(2,1)S(1)}, u32[]{:S(2)}, u32[]{:S(2)}) collective-permute-start(bf16[256,1024]{1,0:T(8,128)(2,1)S(1)} %collective-permute-done.refs_1_), channel_id=1, source_target_pairs={{1,0},{2,1},{3,2},{0,3},{5,4},{6,5},{7,6},{4,7},{9,8},{10,9},{11,1... | collective-permute-start | bytes 1572872 | tf_op jit(solution)/shard_map/ppermute | solution.py:261
  52.5 8.7 %collective-permute-start.3 = (bf16[192,1024]{1,0:T(8,128)(2,1)S(1)}, bf16[192,1024]{1,0:T(8,128)(2,1)S(1)}, u32[]{:S(2)}, u32[]{:S(2)}) collective-permute-start(bf16[192,1024]{1,0:T(8,128)(2,1)S(1)} %bitcast.7), channel_id=1, source_target_pairs={{0,16},{16,0},{1,17},{17,1},{2,18},{18,2},{3,19},{19,3},{4,20},{20... | collective-permute-start | bytes 1179656 | tf_op jit(solution)/shard_map/ppermute | solution.py:267
